TPU v7x, 128 devices: a whole 4x4x4 slice. The times are simulated.
128 devices in a mesh: grid: 16 (over z_hi, y, core), ao: 8 (over x, z_lo).
Axes of the slice: x: 4, y: 4, z: 4 (z_hi: 2, z_lo: 2; z = z_hi * 2 + z_lo), core: 2. Of those that a mesh axis runs over, the one named last changes fastest.
Arguments:
- trial: bfloat16 [12288, 16, 2, 128], P('ao'), may hold values from -0.15625 to 0.15625
- occupied: bfloat16 [12288, 2, 128], P('ao'), may hold values from -0.15625 to 0.15625
- colloc: bfloat16 [64, 128, 1536], P('grid'), may hold values from -3 to 3
- blocks: int32 [64, 12], P('grid'), may hold values from 0 to 95, as said below
- coords: float32 [64, 3, 128], P('grid'), may hold values from 0 to 4
- weights: float32 [64, 128], P('grid'), may hold values from 0.02 to 0.2
Outputs:
- exchange: float32 [16, 12288, 2, 128], P('ao', 'grid')
Inputs may be any that keep to these rules, and one draw needn't show every extreme that they name: The 12 blocks of a batch are distinct and lie among 24 cyclically consecutive shell blocks.
All inputs are finite; a program needn't handle non-finite values.
Results may differ from a plain program's by a relative error of at most 0.0053.
Values may be sent and summed in bfloat16 or wider, within the bound.
A program may use at most 128 MiB of HBM per device.

v0:
```python
import jax
import jax.numpy as jnp
from jax import lax
from jax.sharding import PartitionSpec as P

BLK = 128
NOCC = 128
P_SIZE = 128
SIG = 12


def kernel_matrix(points, quad):
    differ = points[:, :, None] - points[:, None, :]
    square = jnp.sum(differ * differ, axis=0)
    return quad[:, None] * quad[None, :] / jnp.sqrt(square + 0.25)


def pair_exchange(lg_half, og_half, kernel):
    lreal = lg_half[:, :, 0]
    limag = lg_half[:, :, 1]
    oreal = og_half[:, 0]
    oimag = og_half[:, 1]
    f32 = jnp.float32
    rho_real = jnp.einsum("gvi,hi->vgh", lreal, oreal, preferred_element_type=f32) + jnp.einsum(
        "gvi,hi->vgh", limag, oimag, preferred_element_type=f32
    )
    rho_imag = jnp.einsum("gvi,hi->vgh", limag, oreal, preferred_element_type=f32) - jnp.einsum(
        "gvi,hi->vgh", lreal, oimag, preferred_element_type=f32
    )
    m_real = (rho_real * kernel[None]).astype(jnp.bfloat16)
    m_imag = (rho_imag * kernel[None]).astype(jnp.bfloat16)
    e_real = jnp.einsum("vgh,hj->gvj", m_real, oreal, preferred_element_type=f32) - jnp.einsum(
        "vgh,hj->gvj", m_imag, oimag, preferred_element_type=f32
    )
    e_imag = jnp.einsum("vgh,hj->gvj", m_real, oimag, preferred_element_type=f32) + jnp.einsum(
        "vgh,hj->gvj", m_imag, oreal, preferred_element_type=f32
    )
    return jnp.stack([e_real, e_imag], axis=2).astype(jnp.bfloat16)


def project_back(values, potential):
    return lax.dot_general(
        values, potential, (((0,), (0,)), ((), ())), preferred_element_type=jnp.float32
    )


def on_device(trial, occupied, colloc, blocks, coords, weights):
    ao_index = lax.axis_index("ao")
    local_rows = trial.shape[0]
    nblk_local = local_rows // BLK
    nvec_all = trial.shape[1]
    width = nvec_all * 2 * NOCC
    nvec_mine = nvec_all // lax.axis_size("ao")
    nblk_total = nblk_local * lax.axis_size("ao")
    batches = colloc.shape[0]
    combined = jnp.concatenate(
        [trial.reshape(local_rows, width), occupied.reshape(local_rows, 2 * NOCC)], axis=1
    )
    combined = combined.reshape(nblk_local, BLK, width + 2 * NOCC)

    def density(batch_items):
        values, block_ids = batch_items
        local_ids = block_ids - ao_index * nblk_local
        inside = (local_ids >= 0) & (local_ids < nblk_local)
        picked = combined[jnp.clip(local_ids, 0, nblk_local - 1)] * inside[:, None, None].astype(
            jnp.bfloat16
        )
        return jnp.dot(
            values, picked.reshape(SIG * BLK, width + 2 * NOCC), preferred_element_type=jnp.float32
        )

    partial_dens = lax.map(density, (colloc, blocks))
    summed = lax.psum(partial_dens, "ao")
    trial_dens = summed[:, :, :width].reshape(batches, P_SIZE, nvec_all, 2 * NOCC)
    trial_dens = lax.dynamic_slice_in_dim(trial_dens, ao_index * nvec_mine, nvec_mine, 2)
    occ_dens = summed[:, :, width:]
    lg_all = trial_dens.reshape(batches, P_SIZE, nvec_mine, 2, NOCC).astype(jnp.bfloat16)
    og_all = occ_dens.reshape(batches, P_SIZE, 2, NOCC).astype(jnp.bfloat16)

    def potential_of(batch_items):
        lg_half, og_half, points, quad = batch_items
        return pair_exchange(lg_half, og_half, kernel_matrix(points, quad)).reshape(
            P_SIZE, nvec_mine * 2 * NOCC
        )

    potentials = lax.map(potential_of, (lg_all, og_all, coords, weights))
    mine_width = nvec_mine * 2 * NOCC
    nown = nblk_total // lax.axis_size("grid")

    def add_batch(running, batch_items):
        values, block_ids, potential = batch_items
        contrib = project_back(values, potential).reshape(SIG, BLK, mine_width)
        return (running.at[block_ids].add(contrib), None)

    panel, _ = lax.scan(
        add_batch,
        jnp.zeros((nblk_total, BLK, mine_width), jnp.float32),
        (colloc, blocks, potentials),
    )
    owned_rows = lax.psum_scatter(panel, "grid", scatter_dimension=0, tiled=True)
    return owned_rows.reshape(nown * BLK, nvec_mine, 2, NOCC).transpose(1, 0, 2, 3)


def solution(mesh):
    in_specs = (
        P("ao", None, None, None),
        P("ao", None, None),
        P("grid", None, None),
        P("grid", None),
        P("grid", None, None),
        P("grid", None),
    )
    out_specs = P("ao", "grid", None, None)
    return jax.shard_map(
        on_device, mesh=mesh, in_specs=in_specs, out_specs=out_specs, check_vma=False
    )
```

profile of v0, /device:TPU:6, one launch (start us, length us, event | category | flops | bytes accessed | tf_op | source)
XLA Modules:
  0.0 801.8 jit_solution(5183806877886662567)
XLA Ops:
  6.5 2.4 concatenate.9
  9.0 21.1 %concatenate.8 = bf16[12,128,4096]{2,1,0:T(8,128)(2,1)} reshape(bf16[1536,16,2,128]{3,2,1,0:T(2,128)(2,1)} %param.12) | data formatting | bytes 25165824 | tf_op jit(solution)/shard_map/concatenate | solution.py:56
  30.1 10.8 %pad_maximum_fusion.1 = bf16[12,128,4352]{2,1,0:T(8,128)(2,1)} fusion(bf16[12,128,256]{2,1,0:T(8,128)(2,1)S(1)} %concatenate.9, bf16[12,128,4096]{2,1,0:T(8,128)(2,1)} %concatenate.8), kind=kLoop, calls=%fused_computation.56 | loop fusion | flops 26738688 | bytes 26738688 | tf_op jit(solution)/shard_map/concatenate | solution.py:56
  40.9 134.7 %while.32 = (s32[]{:T(128)}, f32[4,128,4352]{1,2,0:T(8,128)}, bf16[4,128,1536]{2,1,0:T(8,128)(2,1)}, s32[4,12]{1,0:T(4,128)S(1)}, s32[]{:T(128)}, /*index=5*/bf16[12,128,4352]{2,1,0:T(8,128)(2,1)}, s32[]{:T(128)}) while((s32[]{:T(128)}, f32[4,128,4352]{1,2,0:T(8,128)}, bf16[4,128,1536]{2,1,0:T(8,128)(2,1)}, s32[4,12]{1,0:T(4,128)S(1)}, ...), condition=%wide.region_1.2_spmd, body=%wide.region_0.1_spmd.sunk | while | flops 1717961856 | bytes 69473664 | solution.py:72
  40.9 11.0 %gather_fusion = bf16[12,128,4352]{2,1,0:T(8,128)(2,1)} fusion(bf16[12,128,4352]{2,1,0:T(8,128)(2,1)} %get-tuple-element.324, s32[1024]{0:T(1024)S(1)} %pad_clamp_fusion.2), kind=kCustom, calls=%fused_computation.clone.1 | custom fusion | bytes 26738736 | tf_op jit(solution)/shard_map/while/body/eval_jaxpr/gather | solution.py:65
  51.9 11.1 %broadcast_multiply_fusion.2 = bf16[12,128,4352]{2,1,0:T(8,128)(2,1)} fusion(bf16[12,128,4352]{2,1,0:T(8,128)(2,1)} %gather_fusion, bf16[12]{0:T(256)(128)(2,1)S(1)} %fusion.59), kind=kLoop, calls=%fused_computation.34.clone.1 | loop fusion | flops 6684672 | bytes 26738712 | tf_op jit(solution)/shard_map/while/body/eval_jaxpr/mul | solution.py:65
  63.0 11.6 %fusion.60 = f32[4,128,4352]{1,2,0:T(8,128)} fusion(f32[4,128,4352]{1,2,0:T(8,128)} %get-tuple-element.313, s32[]{:T(128)S(6)} %copy.87, bf16[1536,4352]{1,0:T(8,128)(2,1)} %bitcast.173, bf16[4,128,1536]{2,1,0:T(8,128)(2,1)} %get-tuple-element.321), kind=kOutput, calls=%fused_computation.36.clone.1 | convolution fusion | flops 1711276032 | bytes 15991808 | tf_op jit(solution)/shard_map/while/body/eval_jaxpr/dot_general | solution.py:68
  74.6 11.1 %gather_fusion = bf16[12,128,4352]{2,1,0:T(8,128)(2,1)} fusion(bf16[12,128,4352]{2,1,0:T(8,128)(2,1)} %get-tuple-element.324, s32[1024]{0:T(1024)S(1)} %pad_clamp_fusion.2), kind=kCustom, calls=%fused_computation.clone.1 | custom fusion | bytes 26738736 | tf_op jit(solution)/shard_map/while/body/eval_jaxpr/gather | solution.py:65
  85.6 11.1 %broadcast_multiply_fusion.2 = bf16[12,128,4352]{2,1,0:T(8,128)(2,1)} fusion(bf16[12,128,4352]{2,1,0:T(8,128)(2,1)} %gather_fusion, bf16[12]{0:T(256)(128)(2,1)S(1)} %fusion.59), kind=kLoop, calls=%fused_computation.34.clone.1 | loop fusion | flops 6684672 | bytes 26738712 | tf_op jit(solution)/shard_map/while/body/eval_jaxpr/mul | solution.py:65
  96.7 11.7 %fusion.60 = f32[4,128,4352]{1,2,0:T(8,128)} fusion(f32[4,128,4352]{1,2,0:T(8,128)} %get-tuple-element.313, s32[]{:T(128)S(6)} %copy.87, bf16[1536,4352]{1,0:T(8,128)(2,1)} %bitcast.173, bf16[4,128,1536]{2,1,0:T(8,128)(2,1)} %get-tuple-element.321), kind=kOutput, calls=%fused_computation.36.clone.1 | convolution fusion | flops 1711276032 | bytes 15991808 | tf_op jit(solution)/shard_map/while/body/eval_jaxpr/dot_general | solution.py:68
  108.4 10.8 %gather_fusion = bf16[12,128,4352]{2,1,0:T(8,128)(2,1)} fusion(bf16[12,128,4352]{2,1,0:T(8,128)(2,1)} %get-tuple-element.324, s32[1024]{0:T(1024)S(1)} %pad_clamp_fusion.2), kind=kCustom, calls=%fused_computation.clone.1 | custom fusion | bytes 26738736 | tf_op jit(solution)/shard_map/while/body/eval_jaxpr/gather | solution.py:65
  119.2 11.1 %broadcast_multiply_fusion.2 = bf16[12,128,4352]{2,1,0:T(8,128)(2,1)} fusion(bf16[12,128,4352]{2,1,0:T(8,128)(2,1)} %gather_fusion, bf16[12]{0:T(256)(128)(2,1)S(1)} %fusion.59), kind=kLoop, calls=%fused_computation.34.clone.1 | loop fusion | flops 6684672 | bytes 26738712 | tf_op jit(solution)/shard_map/while/body/eval_jaxpr/mul | solution.py:65
  130.3 11.6 %fusion.60 = f32[4,128,4352]{1,2,0:T(8,128)} fusion(f32[4,128,4352]{1,2,0:T(8,128)} %get-tuple-element.313, s32[]{:T(128)S(6)} %copy.87, bf16[1536,4352]{1,0:T(8,128)(2,1)} %bitcast.173, bf16[4,128,1536]{2,1,0:T(8,128)(2,1)} %get-tuple-element.321), kind=kOutput, calls=%fused_computation.36.clone.1 | convolution fusion | flops 1711276032 | bytes 15991808 | tf_op jit(solution)/shard_map/while/body/eval_jaxpr/dot_general | solution.py:68
  141.9 11.0 %gather_fusion = bf16[12,128,4352]{2,1,0:T(8,128)(2,1)} fusion(bf16[12,128,4352]{2,1,0:T(8,128)(2,1)} %get-tuple-element.324, s32[1024]{0:T(1024)S(1)} %pad_clamp_fusion.2), kind=kCustom, calls=%fused_computation.clone.1 | custom fusion | bytes 26738736 | tf_op jit(solution)/shard_map/while/body/eval_jaxpr/gather | solution.py:65
  152.9 11.1 %broadcast_multiply_fusion.2 = bf16[12,128,4352]{2,1,0:T(8,128)(2,1)} fusion(bf16[12,128,4352]{2,1,0:T(8,128)(2,1)} %gather_fusion, bf16[12]{0:T(256)(128)(2,1)S(1)} %fusion.59), kind=kLoop, calls=%fused_computation.34.clone.1 | loop fusion | flops 6684672 | bytes 26738712 | tf_op jit(solution)/shard_map/while/body/eval_jaxpr/mul | solution.py:65
  164.0 11.6 %fusion.60 = f32[4,128,4352]{1,2,0:T(8,128)} fusion(f32[4,128,4352]{1,2,0:T(8,128)} %get-tuple-element.313, s32[]{:T(128)S(6)} %copy.87, bf16[1536,4352]{1,0:T(8,128)(2,1)} %bitcast.173, bf16[4,128,1536]{2,1,0:T(8,128)(2,1)} %get-tuple-element.321), kind=kOutput, calls=%fused_computation.36.clone.1 | convolution fusion | flops 1711276032 | bytes 15991808 | tf_op jit(solution)/shard_map/while/body/eval_jaxpr/dot_general | solution.py:68
  175.6 343.8 %all-reduce.1 = bf16[4,128,4352]{1,2,0:T(8,128)(2,1)} all-reduce(f32[4,128,4352]{1,2,0:T(8,128)} %get-tuple-element.136), channel_id=1, replica_groups=mesh['grid'=16,'ao'=8] {'ao'}, use_global_device_ids=true, to_apply=%region_2.3 | all-reduce | flops 2228224 | bytes 13369344 | tf_op jit(solution)/shard_map/psum | solution.py:73
  519.3 1.0 slice.46
  520.3 4.4 slice.28
  524.7 1.1 dynamic-slice_convert_fusion
  525.8 16.9 %while.33 = (s32[]{:T(128)}, bf16[4,128,512]{1,2,0:T(8,128)(2,1)}, bf16[4,128,2,128]{1,3,2,0:T(8,128)(2,1)S(1)}, bf16[4,128,2,2,128]{1,4,3,2,0:T(8,128)(2,1)S(1)...) while((s32[]{:T(128)}, bf16[4,128,512]{1,2,0:T(8,128)(2,1)}, ...), condition=%wide.region_5.6_spmd, body=%wide.region_3.5_spmd.sunk | while | flops 67682304 | bytes 4138089 | solution.py:86
  525.8 0.7 fusion.66
  526.5 0.7 constant_dynamic-slice_fusion.13
  529.4 0.7 constant_dynamic-update-slice_fusion.2
  530.0 0.7 fusion.66
  530.7 0.7 constant_dynamic-slice_fusion.13
  533.6 0.7 constant_dynamic-update-slice_fusion.2
  534.2 0.7 fusion.66
  534.9 0.7 constant_dynamic-slice_fusion.13
  538.5 0.7 fusion.66
  539.1 0.7 constant_dynamic-slice_fusion.13
  542.7 11.5 %broadcast_in_dim.15 = f32[96,128,512]{2,1,0:T(8,128)} broadcast(f32[]{:T(128)} %constant.71.clone.1), dimensions={} | broadcast | bytes 25165828 | tf_op jit(solution)/shard_map/broadcast_in_dim | solution.py:97
  554.2 42.7 %while.34 = (s32[]{:T(128)}, f32[96,128,512]{2,1,0:T(8,128)}, s32[4,12]{1,0:T(4,128)S(1)}, bf16[4,128,1536]{2,1,0:T(8,128)(2,1)}, bf16[4,128,512]{1,2,0:T(8,128)(2,1)}, /*index=5*/s32[]{:T(128)}) while((s32[]{:T(128)}, f32[96,128,512]{2,1,0:T(8,128)}, s32[4,12]{1,0:T(4,128)S(1)}, bf16[4,128,1536]{2,1,0:T(8,128)(2,1)}, ...), condition=%wide.region_8.9_spmd, body=%wide.region_6.8_spmd.sunk | while | flops 202113056 | bytes 14680297 | solution.py:95
  554.2 1.0 constant_dynamic-slice_fusion.14
  555.5 1.5 fusion.77
  556.9 8.0 %scatter_fusion = f32[96,128,512]{2,1,0:T(8,128)} fusion(f32[96,128,512]{2,1,0:T(8,128)} %get-tuple-element.354, s32[12]{0:T(128)S(1)} %fusion.76, f32[12,128,512]{2,1,0:T(8,128)S(1)} %fusion.77), kind=kCustom, calls=%fused_computation.1.clone.1 | custom fusion | flops 786432 | bytes 9437232 | tf_op jit(solution)/shard_map/while/body/eval_jaxpr/scatter-add | solution.py:93
  565.0 1.0 constant_dynamic-slice_fusion.14
  566.2 1.5 fusion.77
  567.7 7.9 scatter_fusion
  575.6 1.0 constant_dynamic-slice_fusion.14
  576.8 1.5 fusion.77
  578.3 8.0 scatter_fusion
  586.3 1.0 constant_dynamic-slice_fusion.14
  587.6 1.5 fusion.77
  589.1 7.9 scatter_fusion
  597.0 194.0 %reduce-scatter.2.cloned.1.call-done = f32[6,128,512]{2,1,0:T(8,128)} async-done(((f32[96,128,512]{2,1,0:T(8,128)}), f32[6,128,512]{2,1,0:T(8,128)}) %reduce-scatter.2.cloned.1.call-update) | async-done | bytes 1572880 | tf_op jit(solution)/shard_map/reduce_scatter | solution.py:100
  791.0 2.3 reshape.186
  793.3 1.7 copy.48
  (100 shorter events, 10.7 us)
Async XLA Ops:
  6.5 784.5 %reduce-scatter.2.cloned.1.call-start = ((), (), s32[]{:S(2)}) async-start(), calls=%async_computation.1 | async-start | bytes 26738688 | tf_op jit(solution)/shard_map/reduce_scatter | solution.py:100
  30.1 10.8 %copy-start = (s32[4,12]{1,0:T(4,128)S(1)}, s32[4,12]{1,0:T(4,128)}, u32[]{:S(2)}) copy-start(s32[4,12]{1,0:T(4,128)} %param.15) | copy-start | bytes 580
Sparse Core Ops, SparseCore 0:
  597.1 193.8 reduce-scatter.1
where the time goes:
time: 804 us; the launch traced here: 802 us
  blocking collectives  344 us (43%)
  waiting for transfers between devices  194 us (24%)
  local copies, waits for them, and re-layouts  104 us (13%)
  other arithmetic  87.8 us (11%)
  matrix products  58.2 us (7%)
  between operations  13.4 us (2%)
    psum x1, blocking collectives, on_device(): summed = lax.psum(partial_dens, 'ao')  344 us
    reduce_scatter x1, waiting for transfers between devices, on_device(): lax.psum_scatter(panel, 'grid', scatter_dimension=0, tiled=True)  194 us
    dot_general x4, matrix products, density(): jnp.dot(values, picked.reshape(SIG * BLK, width + 2 * NOCC), preferred_el...  46.4 us
    mul x4, other arithmetic, density(): combined[jnp.clip(local_ids, 0, nblk_local - 1)]  44.2 us
    gather x4, local copies, waits for them, and re-layouts, density(): combined[jnp.clip(local_ids, 0, nblk_local - 1)]  43.8 us
    scatter-add x4, other arithmetic, add_batch(): return (running.at[block_ids].add(contrib), None)  31.8 us
    concatenate x2, local copies, waits for them, and re-layouts, on_device(): jnp.concatenate([trial.reshape(local_rows, width), occupied.reshape(local...  23.6 us
  transfers between devices with their start and end apart: 1, of which 1 were waited for; matrix products, arithmetic and copies ran while one was open for 0% of the time, Pallas kernels for 0%

commit v1 on v0

v1 whole, which is shorter than its diff:
```python
import functools
import jax
import jax.numpy as jnp
from jax import lax
from jax.experimental import pallas as pl
from jax.experimental.pallas import tpu as pltpu
from jax.sharding import PartitionSpec as P

BLK = 128
NOCC = 128
SIG = 12
F32 = jnp.float32
BF16 = jnp.bfloat16
MESH = pl.DeviceIdType.MESH
ROWS = 512


def coords_of():
    g = lax.axis_index("grid")
    a = lax.axis_index("ao")
    return g // 8, lax.rem(g // 2, 4), lax.rem(g, 2), a // 2, lax.rem(a, 2)


def device_at(zh, y, c, x, zl):
    return (zh * 8 + y * 2 + c, x * 2 + zl)


def prep_kernel(idx_ref, x_ref, occ_ref, xloc_ref, od_ref, w):
    nloc = xloc_ref.shape[1] // BLK
    for k in range(0, w.shape[0], 256):
        both = occ_ref[k : k + 256].astype(F32)
        w[k : k + 256, :NOCC] = both[:, 0, :].astype(BF16)
        w[k : k + 256, NOCC:] = both[:, 1, :].astype(BF16)
    for b in range(4):
        for l in range(nloc):
            s = idx_ref[b, l]
            at = pl.multiple_of(jnp.minimum(s, SIG - 1) * BLK, BLK)
            tile = x_ref[b, :, pl.ds(at, BLK)]
            xloc_ref[b * BLK : (b + 1) * BLK, l * BLK : (l + 1) * BLK] = jnp.where(
                s < SIG, tile, jnp.zeros_like(tile)
            )
    od_ref[...] = jnp.dot(xloc_ref[...], w[...], preferred_element_type=F32)


def prep(idx, colloc, occupied):
    rows = occupied.shape[0]
    return pl.pallas_call(
        prep_kernel,
        out_shape=(
            jax.ShapeDtypeStruct((ROWS, rows), BF16),
            jax.ShapeDtypeStruct((ROWS, 2 * NOCC), F32),
        ),
        in_specs=[
            pl.BlockSpec(memory_space=pltpu.SMEM),
            pl.BlockSpec(memory_space=pltpu.VMEM),
            pl.BlockSpec(memory_space=pltpu.VMEM),
        ],
        out_specs=(pl.BlockSpec(memory_space=pltpu.VMEM),) * 2,
        scratch_shapes=[pltpu.VMEM((rows, 2 * NOCC), BF16)],
        compiler_params=pltpu.CompilerParams(vmem_limit_bytes=40 << 20),
        name="prep",
    )(idx, colloc, occupied)


class GatherY:
    def __init__(self, own, slots, send, recv, local):
        self.own, self.slots = own, slots
        self.send, self.recv, self.local = send, recv, local
        zh, y, c, x, zl = coords_of()
        self.right = device_at(zh, lax.rem(y + 1, 4), c, x, zl)
        self.left = device_at(zh, lax.rem(y + 3, 4), c, x, zl)
        self.twin = device_at(zh, y, 1 - c, x, zl)

    def copy(self, n, src, dst, to):
        return pltpu.make_async_remote_copy(
            src_ref=src, dst_ref=dst, send_sem=self.send.at[n], recv_sem=self.recv.at[n],
            device_id=to, device_id_type=MESH,
        )

    def at(self, n):
        s, own = self.slots, self.own
        lo, hi = pl.ds(0, 2), pl.ds(2, 2)
        src, dst, to = [
            (own, s.at[0, 1], self.right),
            (own, s.at[0, 2], self.left),
            (own, s.at[1, 0], self.twin),
            (s.at[0, 1, lo], s.at[0, 3, lo], self.right),
            (s.at[0, 2, hi], s.at[0, 3, hi], self.left),
            (s.at[0, 1], s.at[1, 1], self.twin),
            (s.at[0, 2], s.at[1, 2], self.twin),
            (s.at[0, 3], s.at[1, 3], self.twin),
        ][n]
        return self.copy(n, src, dst, to)

    def keep(self):
        return pltpu.make_async_copy(self.own, self.slots.at[0, 0], self.local)

    def start(self):
        for n in (0, 1, 2):
            self.at(n).start()
        self.keep().start()

    def forward(self):
        self.at(0).wait_recv()
        self.at(3).start()
        self.at(5).start()
        self.at(1).wait_recv()
        self.at(4).start()
        self.at(6).start()

    def finish(self):
        self.at(3).wait_recv()
        self.at(4).wait_recv()
        self.at(7).start()
        for n in (2, 5, 6, 7):
            self.at(n).wait_recv()
        for n in range(8):
            self.at(n).wait_send()
        self.keep().wait()


def greet(peers):
    barrier = pltpu.get_barrier_semaphore()
    for peer in peers:
        pl.semaphore_signal(barrier, inc=1, device_id=peer, device_id_type=MESH)
    pl.semaphore_wait(barrier, len(peers))


def density_kernel(
    trial_ref, xloc_ref, x_ref, lg_ref, xall_ref,
    buf, w, opp, part, own, rec1, rec2, zsend, zrec,
    load_sem, send, recv, gsend, grecv, glocal,
):
    zh, y, c, x, zl = coords_of()
    right = device_at(zh, y, c, lax.rem(x + 1, 4), zl)
    left = device_at(zh, y, c, lax.rem(x + 3, 4), zl)
    across = device_at(zh, y, c, x, 1 - zl)
    order = [lax.rem(x + d, 4) for d in (2, 1, 3, 0)]
    gather = GatherY(x_ref, xall_ref, gsend, grecv, glocal)

    def load(v):
        return pltpu.make_async_copy(trial_ref.at[:, v], buf.at[v], load_sem.at[v])

    for dest in order:
        for t in range(4):
            load(dest * 4 + t).start()

    greet([right, left, across, gather.right, gather.left, gather.twin])
    gather.start()

    def densities(dest, store):
        def one(t, _):
            v = dest * 4 + t
            load(v).wait()

            def split(k, _):
                k = pl.multiple_of(k * 256, 256)
                both = buf[v, pl.ds(k, 256)].astype(F32)
                w[pl.ds(k, 256), :NOCC] = both[:, 0, :].astype(BF16)
                w[pl.ds(k, 256), NOCC:] = both[:, 1, :].astype(BF16)
                return 0

            lax.fori_loop(0, w.shape[0] // 256, split, 0)
            store(
                pl.ds(pl.multiple_of(t * 256, 256), 256),
                jnp.dot(xloc_ref[...], w[...], preferred_element_type=F32),
            )
            return 0

        lax.fori_loop(0, 4, one, 0)

    def remote(n, src, dst, to):
        return pltpu.make_async_remote_copy(
            src_ref=src, dst_ref=dst, send_sem=send.at[n], recv_sem=recv.at[n],
            device_id=to, device_id_type=MESH,
        )

    lo, hi = pl.ds(0, 256), pl.ds(256, 256)
    copies = [
        remote(0, opp.at[lo], rec1.at[0], right),
        remote(1, opp.at[hi], rec1.at[1], left),
        remote(2, part.at[0, hi], rec2.at[0, hi], right),
        remote(3, part.at[1, lo], rec2.at[1, lo], left),
        remote(4, part.at[0, lo], rec2.at[0, lo], right),
        remote(5, part.at[1, hi], rec2.at[1, hi], left),
        remote(6, zsend, zrec, across),
    ]

    def store_opp(cols, value):
        opp[:, cols] = value.astype(BF16)

    def store_right(cols, value):
        own[lo, cols] = value[:256]
        part[0, hi, cols] = value[256:].astype(BF16)

    def store_left(cols, value):
        part[1, lo, cols] = value[:256].astype(BF16)
        own[hi, cols] = value[256:]

    def store_own(cols, value):
        own[:, cols] = value

    densities(order[0], store_opp)
    copies[0].start()
    copies[1].start()
    densities(order[1], store_right)
    copies[2].start()
    copies[0].wait_recv()

    def add_right(i, _):
        r = pl.ds(pl.multiple_of(i * 16, 16), 16)
        part[0, r] = (own[r] + rec1[0, r].astype(F32)).astype(BF16)
        return 0

    lax.fori_loop(0, 16, add_right, 0)
    copies[4].start()
    densities(order[2], store_left)
    copies[3].start()
    copies[1].wait_recv()

    def add_left(i, _):
        r = pl.ds(pl.multiple_of(i * 16, 16), 16)
        q = pl.ds(pl.multiple_of(256 + i * 16, 16), 16)
        part[1, q] = (own[q] + rec1[1, r].astype(F32)).astype(BF16)
        return 0

    lax.fori_loop(0, 16, add_left, 0)
    copies[5].start()
    densities(order[3], store_own)
    gather.forward()
    for n in (2, 3, 4, 5):
        copies[n].wait_recv()

    theirs = pl.ds(pl.multiple_of((1 - zl) * 512, 512), 512)
    mine = pl.ds(pl.multiple_of(zl * 512, 512), 512)

    def total(r, cols):
        return own[r, cols] + rec2[0, r, cols].astype(F32) + rec2[1, r, cols].astype(F32)

    def give(i, _):
        r = pl.ds(pl.multiple_of(i * 16, 16), 16)
        zsend[r] = total(r, theirs).astype(BF16)
        return 0

    lax.fori_loop(0, 32, give, 0)
    copies[6].start()
    copies[6].wait_recv()

    def last(i, _):
        r = pl.ds(pl.multiple_of(i * 16, 16), 16)
        lg_ref[r] = (total(r, mine) + zrec[r].astype(F32)).astype(BF16)
        return 0

    lax.fori_loop(0, 32, last, 0)
    gather.finish()
    for n in range(7):
        copies[n].wait_send()


def density(trial, xloc, colloc):
    rows = trial.shape[0]
    hbm = pl.BlockSpec(memory_space=pl.ANY)
    vmem = pl.BlockSpec(memory_space=pltpu.VMEM)
    return pl.pallas_call(
        density_kernel,
        out_shape=(
            jax.ShapeDtypeStruct((ROWS, 512), BF16),
            jax.ShapeDtypeStruct((2, 4) + colloc.shape, BF16),
        ),
        in_specs=[hbm, vmem, hbm],
        out_specs=(vmem, hbm),
        scratch_shapes=[
            pltpu.VMEM((16, rows, 2, NOCC), BF16),
            pltpu.VMEM((rows, 256), BF16),
            pltpu.VMEM((ROWS, 1024), BF16),
            pltpu.VMEM((2, ROWS, 1024), BF16),
            pltpu.VMEM((ROWS, 1024), F32),
            pltpu.VMEM((2, 256, 1024), BF16),
            pltpu.VMEM((2, ROWS, 1024), BF16),
            pltpu.VMEM((ROWS, 512), BF16),
            pltpu.VMEM((ROWS, 512), BF16),
            pltpu.SemaphoreType.DMA((16,)),
            pltpu.SemaphoreType.DMA((7,)),
            pltpu.SemaphoreType.DMA((7,)),
            pltpu.SemaphoreType.DMA((8,)),
            pltpu.SemaphoreType.DMA((8,)),
            pltpu.SemaphoreType.DMA,
        ],
        compiler_params=pltpu.CompilerParams(
            vmem_limit_bytes=56 << 20, collective_id=0, has_side_effects=True
        ),
        cost_estimate=pl.CostEstimate(
            flops=7 * 10**9, bytes_accessed=150 * 10**6, transcendentals=0
        ),
        name="density",
    )(trial, xloc, colloc)


def pair_kernel(lg_ref, og_ref, kern_ref, eall_ref, e, send, recv, local):
    gather = GatherY(e, eall_ref, send, recv, local)
    for b in range(4):
        r = pl.ds(b * BLK, BLK)
        ore = og_ref[r, :NOCC]
        oim = og_ref[r, NOCC:]
        w = jnp.concatenate(
            [
                jnp.concatenate([ore, oim], axis=1),
                jnp.concatenate([-oim, ore], axis=1),
            ],
            axis=0,
        ).astype(BF16)
        kern = kern_ref[b]
        both = jnp.concatenate([kern, kern], axis=1)
        for v in range(2):
            cols = pl.ds(v * 256, 256)
            rho = lax.dot_general(
                lg_ref[r, cols], w, (((1,), (1,)), ((), ())), preferred_element_type=F32
            )
            m = (rho * both).astype(BF16)
            e[b, :, cols] = jnp.dot(m, w, preferred_element_type=F32).astype(BF16)
    greet([gather.right, gather.left, gather.twin])
    gather.start()
    gather.forward()
    gather.finish()


def pair(lg, og, kern):
    vmem = pl.BlockSpec(memory_space=pltpu.VMEM)
    return pl.pallas_call(
        pair_kernel,
        out_shape=jax.ShapeDtypeStruct((2, 4, 4, BLK, 512), BF16),
        in_specs=[vmem] * 3,
        out_specs=vmem,
        scratch_shapes=[
            pltpu.VMEM((4, BLK, 512), BF16),
            pltpu.SemaphoreType.DMA((8,)),
            pltpu.SemaphoreType.DMA((8,)),
            pltpu.SemaphoreType.DMA,
        ],
        compiler_params=pltpu.CompilerParams(
            vmem_limit_bytes=40 << 20, collective_id=1, has_side_effects=True
        ),
        name="pair",
    )(lg, og, kern)


def panel_kernel(idx_ref, x_ref, e_ref, keep_ref, give_ref, acc):
    def row(r, _):
        acc[...] = jnp.zeros_like(acc)

        def batch(j, _):
            s = idx_ref[r, j]

            @pl.when(s < SIG)
            def _():
                at = pl.multiple_of(s * BLK, BLK)
                acc[...] += lax.dot_general(
                    x_ref[j, :, pl.ds(at, BLK)], e_ref[j], (((0,), (0,)), ((), ())),
                    preferred_element_type=F32,
                )

            return 0

        lax.fori_loop(0, 32, batch, 0)

        @pl.when(r < 6)
        def _():
            keep_ref[jnp.minimum(r, 5)] = acc[...]

        @pl.when(r >= 6)
        def _():
            give_ref[jnp.maximum(r - 6, 0)] = acc[...].astype(BF16)

        return 0

    lax.fori_loop(0, 12, row, 0)


def panel(idx, xall, eall):
    vmem = pl.BlockSpec(memory_space=pltpu.VMEM)
    return pl.pallas_call(
        panel_kernel,
        out_shape=(
            jax.ShapeDtypeStruct((6, BLK, 512), F32),
            jax.ShapeDtypeStruct((6, BLK, 512), BF16),
        ),
        in_specs=[pl.BlockSpec(memory_space=pltpu.SMEM), vmem, vmem],
        out_specs=(vmem, vmem),
        scratch_shapes=[pltpu.VMEM((BLK, 512), F32)],
        compiler_params=pltpu.CompilerParams(vmem_limit_bytes=48 << 20),
        name="panel",
    )(idx, xall, eall)


def place_of(ids, wanted):
    hit = ids[..., None, :] == wanted[..., :, None]
    where = jnp.arange(SIG, dtype=jnp.int32)
    return SIG + jnp.sum(jnp.where(hit, where - SIG, 0), axis=-1).astype(jnp.int32)


def on_device(trial, occupied, colloc, blocks, coords, weights):
    zh, y, c, x, zl = coords_of()
    a = lax.axis_index("ao")
    g = lax.axis_index("grid")
    nloc = trial.shape[0] // BLK
    local = a * nloc + jnp.arange(nloc, dtype=jnp.int32)
    xloc, od = prep(place_of(blocks, local), colloc, occupied)
    og = lax.psum(od, "ao")

    table = lax.all_gather(blocks, "grid").reshape(2, 4, 2, 4, SIG)
    lg, xall = density(trial, xloc, colloc)

    differ = coords[:, :, :, None] - coords[:, :, None, :]
    square = jnp.sum(differ * differ, axis=1)
    kern = weights[:, :, None] * weights[:, None, :] / jnp.sqrt(square + 0.25)
    eall = pair(lg, og.astype(BF16), kern)

    half = lax.dynamic_index_in_dim(table, zh, 0, keepdims=False)
    ys = lax.rem(y + jnp.array([0, 3, 1, 2], jnp.int32), 4)
    cs = jnp.stack([c, 1 - c])
    ids = half[ys][:, cs].transpose(1, 0, 2, 3).reshape(32, SIG)
    step = jnp.arange(6, dtype=jnp.int32)
    first = (y * 2 + c) * 6
    rows = jnp.concatenate([zh * 48 + first + step, (1 - zh) * 48 + first + step])
    idx = place_of(ids, rows).T
    keep, give = panel(
        idx, xall.reshape(32, BLK, SIG * BLK), eall.reshape(32, BLK, 512)
    )
    n = lax.axis_size("grid")
    got = lax.ppermute(give, "grid", [(i, (i + n // 2) % n) for i in range(n)])
    total = keep + got.astype(F32)
    return total.reshape(6 * BLK, 2, 2, NOCC).transpose(1, 0, 2, 3)


def solution(mesh):
    in_specs = (
        P("ao", None, None, None),
        P("ao", None, None),
        P("grid", None, None),
        P("grid", None),
        P("grid", None, None),
        P("grid", None),
    )
    out_specs = P("ao", "grid", None, None)
    return jax.shard_map(
        on_device, mesh=mesh, in_specs=in_specs, out_specs=out_specs, check_vma=False
    )
```

time: 804 us -> 219 us (0.27)
  the two profiles are of different devices: /device:TPU:6 before, /device:TPU:31 now
where the time goes in v1:
time: 219 us
  Pallas kernels  133 us (61%)
  blocking collectives  51.4 us (23%)
  waiting for transfers between devices  19.1 us (9%)
  local copies, waits for them, and re-layouts  11.4 us (5%)
  other arithmetic  2.63 us (1%)
    pallas_call x1, Pallas kernels, density(): pl.pallas_call(density_kernel, out_shape=(jax.ShapeDtypeStruct((ROWS, 512...  71.2 us
    pallas_call x1, Pallas kernels, pair(): pl.pallas_call(pair_kernel, out_shape=jax.ShapeDtypeStruct((2, 4, 4, BLK,...  36.4 us
    psum x1, blocking collectives, on_device(): og = lax.psum(od, 'ao')  31.8 us
    pallas_call x1, Pallas kernels, panel(): pl.pallas_call(panel_kernel, out_shape=(jax.ShapeDtypeStruct((6, BLK, 512...  23.2 us
    all_gather x1, blocking collectives, on_device(): table = lax.all_gather(blocks, 'grid').reshape(2, 4, 2, 4, SIG)  19.6 us
    ppermute x1, waiting for transfers between devices, on_device(): got = lax.ppermute(give, 'grid', [(i, (i + n // 2) % n) for i in range(n)])  19.1 us
    unnamed x13, local copies, waits for them, and re-layouts  7.36 us
  transfers between devices with their start and end apart: 1, of which 1 were waited for; matrix products, arithmetic and copies ran while one was open for 0% of the time, Pallas kernels for 0%

profile of v1, /device:TPU:31, one launch (start us, length us, event | category | flops | bytes accessed | tf_op | source)
XLA Modules:
  0.0 218.5 jit_solution(1186927097523306660)
XLA Ops:
  0.0 0.7 compare_select_fusion.1
  0.7 0.1 fusion.1
  0.8 1.0 select_reduce_fusion.1
  1.8 0.1 copy.19
  1.9 0.7 copy.20
  2.6 19.6 %all-gather.1 = s32[16,4,12]{2,1,0:T(4,128)S(1)} all-gather(s32[1,4,12]{2,1,0:T(4,128)} %bitcast.20), channel_id=2, replica_groups=mesh['grid'=16,'ao'=8] {'grid'}, dimensions={0}, use_global_device_ids=true | all-gather | bytes 3264 | tf_op jit(solution)/shard_map/all_gather | solution.py:410
  22.2 0.6 gather_fusion
  22.8 0.6 gather_fusion.1
  23.4 0.1 copy.18
  23.4 0.1 pad_add_fusion
  23.5 0.1 select_reduce_fusion
  23.7 0.3 multiply_reduce_fusion
  23.9 0.0 copy-start.1
  23.9 1.4 copy-done.1
  25.3 0.0 copy-start.2
  25.4 1.1 copy-done.2
  26.5 0.0 copy-start.5
  26.5 2.6 %prep.1 = (bf16[512,1536]{1,0:T(8,128)(2,1)S(1)}, f32[512,256]{1,0:T(8,128)S(1)}) custom-call(s32[4,12]{1,0:T(4,128)S(1)} %broadcast_add_fusion.idx_ref, bf16[4,128,1536]{2,1,0:T(8,128)(2,1)S(1)} %copy-done.1, bf16[1536,2,128]{2,1,0:T(2,128)(2,1)S(1)} %copy-done.2), custom_call_target="tpu_custom_call" | custom-call | tf_op jit(solution)/shard_map/prep/pallas_call | solution.py:47
  29.1 0.0 copy-start.4
  29.1 1.1 copy-done.4
  30.2 31.8 %all-reduce.1.og_ref = bf16[512,256]{1,0:T(8,128)(2,1)S(1)} all-reduce(f32[512,256]{1,0:T(8,128)S(1)} %get-tuple-element.14), channel_id=1, replica_groups=mesh['grid'=16,'ao'=8] {'ao'}, use_global_device_ids=true, to_apply=%region_2.3 | all-reduce | flops 131072 | bytes 786432 | tf_op jit(solution)/shard_map/psum | solution.py:408
  62.0 0.0 copy-done.5
  62.0 0.1 rsqrt_multiply_fusion.kern_ref
  62.1 71.2 %density.1 = (bf16[512,512]{1,0:T(8,128)(2,1)}, bf16[2,4,4,128,1536]{4,3,2,1,0:T(8,128)(2,1)}) custom-call(bf16[1536,16,2,128]{3,2,1,0:T(2,128)(2,1)} %trial_ref.1, bf16[512,1536]{1,0:T(8,128)(2,1)} %copy-done.4, bf16[4,128,1536]{2,1,0:T(8,128)(2,1)} %x_ref.3), custom_call_target="tpu_custom_call" | custom-call | flops 7000000000 | bytes 150000000 | tf_op jit(solution)/shard_map/density/pallas_call | solution.py:264
  133.4 0.0 copy-start.3
  133.4 1.0 copy-done.3
  134.4 36.4 %pair.1 = bf16[2,4,4,128,512]{4,3,2,1,0:T(8,128)(2,1)S(1)} custom-call(bf16[512,512]{1,0:T(8,128)(2,1)S(1)} %copy-done.3, bf16[512,256]{1,0:T(8,128)(2,1)S(1)} %all-reduce.1.og_ref, f32[4,128,128]{2,1,0:T(8,128)S(1)} %rsqrt_multiply_fusion.kern_ref), custom_call_target="tpu_custom_call" | custom-call | tf_op jit(solution)/shard_map/pair/pallas_call | solution.py:329
  170.8 0.0 copy-start
  170.8 1.9 copy-done
  172.7 23.2 %panel.1 = (f32[6,128,512]{2,1,0:T(8,128)S(1)}, bf16[6,128,512]{2,1,0:T(8,128)(2,1)S(1)}) custom-call(s32[12,32]{1,0:T(8,128)S(1)} %add_bitcast_fusion.idx_ref, bf16[32,128,1536]{2,1,0:T(8,128)(2,1)} %bitcast.17, bf16[32,128,512]{2,1,0:T(8,128)(2,1)} %bitcast.16), custom_call_target="tpu_custom_call" | custom-call | tf_op jit(solution)/shard_map/panel/pallas_call | solution.py:381
  196.0 0.5 collective-permute-start
  196.5 19.1 %collective-permute-done = bf16[6,128,512]{2,1,0:T(8,128)(2,1)S(1)} collective-permute-done((bf16[6,128,512]{2,1,0:T(8,128)(2,1)S(1)}, bf16[6,128,512]{2,1,0:T(8,128)(2,1)S(1)}, u32[]{:S(2)}, u32[]{:S(2)}) %collective-permute-start) | collective-permute-done | bytes 786464 | tf_op jit(solution)/shard_map/ppermute | solution.py:430
  215.6 0.2 convert_add_fusion
  215.8 1.0 reshape.111
  216.8 1.7 copy.24
  (7 shorter events, 0.0 us)
Async XLA Ops:
  23.9 1.4 copy-start.1
  25.3 1.1 copy-start.2
  26.5 35.5 %copy-start.5 = (f32[4,128]{1,0:T(4,128)S(1)}, f32[4,128]{1,0:T(4,128)}, u32[]{:S(2)}) copy-start(f32[4,128]{1,0:T(4,128)} %param.12) | copy-start | bytes 6148
  29.1 1.1 copy-start.4
  133.4 1.0 copy-start.3
  170.8 2.0 copy-start
  196.0 19.6 %collective-permute-start = (bf16[6,128,512]{2,1,0:T(8,128)(2,1)S(1)}, bf16[6,128,512]{2,1,0:T(8,128)(2,1)S(1)}, u32[]{:S(2)}, u32[]{:S(2)}) collective-permute-start(bf16[6,128,512]{2,1,0:T(8,128)(2,1)S(1)} %get-tuple-element.16), channel_id=1, source_target_pairs={{0,64},{8,72},{16,80},{24,88},{32,96},{40,104},{48,112},{56,120},{... | collective-permute-start | bytes 2359304 | tf_op jit(solution)/shard_map/ppermute | solution.py:430

commit v2 on v0

v2 whole, which is shorter than its diff:
```python
import functools
import jax
import jax.numpy as jnp
from jax import lax
from jax.experimental import pallas as pl
from jax.experimental.pallas import tpu as pltpu
from jax.sharding import PartitionSpec as P

BLK = 128
NOCC = 128
SIG = 12
F32 = jnp.float32
BF16 = jnp.bfloat16
MESH = pl.DeviceIdType.MESH
ROWS = 512


def coords_of():
    g = lax.axis_index("grid")
    a = lax.axis_index("ao")
    return g // 8, lax.rem(g // 2, 4), lax.rem(g, 2), a // 2, lax.rem(a, 2)


def device_at(zh, y, c, x, zl):
    return (zh * 8 + y * 2 + c, x * 2 + zl)


class GatherY:
    def __init__(self, own, slots, first, count, base, send, recv):
        self.own, self.slots, self.base = own, slots, base
        self.send, self.recv = send, recv
        half = count // 2
        self.every = pl.ds(first, count)
        self.lo, self.hi = pl.ds(first, half), pl.ds(first + half, half)
        zh, y, c, x, zl = coords_of()
        self.right = device_at(zh, lax.rem(y + 1, 4), c, x, zl)
        self.left = device_at(zh, lax.rem(y + 3, 4), c, x, zl)
        self.twin = device_at(zh, y, 1 - c, x, zl)

    def at(self, n):
        s, own, lo, hi, every = self.slots, self.own, self.lo, self.hi, self.every
        src, dst, to = [
            (own.at[lo], s.at[0, 1, lo], self.right),
            (own.at[hi], s.at[0, 2, hi], self.left),
            (own.at[hi], s.at[0, 1, hi], self.right),
            (own.at[lo], s.at[0, 2, lo], self.left),
            (own.at[every], s.at[1, 0, every], self.twin),
            (s.at[0, 1, lo], s.at[0, 3, lo], self.right),
            (s.at[0, 2, hi], s.at[0, 3, hi], self.left),
            (s.at[0, 1, every], s.at[1, 1, every], self.twin),
            (s.at[0, 2, every], s.at[1, 2, every], self.twin),
            (s.at[0, 3, every], s.at[1, 3, every], self.twin),
        ][n]
        return remote(self.send, self.recv, self.base + n, src, dst, to)

    def start_first(self):
        for n in (0, 1):
            self.at(n).start()

    def start_second(self):
        for n in (2, 3, 4):
            self.at(n).start()

    def forward(self):
        for n in (0, 1):
            self.at(n).wait_recv()
            self.at(n + 5).start()

    def spread(self):
        for n in (2, 3):
            self.at(n).wait_recv()
            self.at(n + 5).start()

    def spread_opposite(self):
        for n in (5, 6):
            self.at(n).wait_recv()
        self.at(9).start()

    def finish(self):
        for n in (4, 7, 8, 9):
            self.at(n).wait_recv()
        for n in range(10):
            self.at(n).wait_send()


def remote(send, recv, n, src, dst, to):
    return pltpu.make_async_remote_copy(
        src_ref=src, dst_ref=dst, send_sem=send.at[n], recv_sem=recv.at[n],
        device_id=to, device_id_type=MESH,
    )


def greet(peers):
    barrier = pltpu.get_barrier_semaphore()
    for peer in peers:
        pl.semaphore_signal(barrier, inc=1, device_id=peer, device_id_type=MESH)
    pl.semaphore_wait(barrier, len(peers))


def rows_of(start, size):
    return pl.ds(pl.multiple_of(start, size), size)


def main_kernel(
    idx_ref, trial_ref, x_ref, occ_ref, ids_ref, kern_ref,
    xall_ref, eall_ref, idall_ref,
    buf, w, xpad, xloc, opp, part, own, rec1, rec2, zsend, zrec, lg, od, orec, og,
    load_sem, send, recv, osend, orecv, gsend, grecv, local,
):
    zh, y, c, x, zl = coords_of()
    a = x * 2 + zl
    right = device_at(zh, y, c, lax.rem(x + 1, 4), zl)
    left = device_at(zh, y, c, lax.rem(x + 3, 4), zl)
    across = device_at(zh, y, c, x, 1 - zl)
    order = [lax.rem(x + d, 4) for d in (2, 1, 3, 0)]

    def load(v):
        return pltpu.make_async_copy(trial_ref.at[:, v], buf.at[v], load_sem.at[v])

    for dest in order:
        for t in range(4):
            load(dest * 4 + t).start()

    ao_peers = [(lax.axis_index("grid"), lax.rem(a + d, 8)) for d in range(1, 8)]
    grid_peers = [
        (device_at(zh, lax.rem(y + d, 4), c if same else 1 - c, x, zl), 0 if same else 1, slot)
        for d, slot in ((0, 0), (1, 1), (3, 2), (2, 3))
        for same in (True, False)
        if d or not same
    ]
    greet(ao_peers + [peer for peer, _, _ in grid_peers])

    gx = GatherY(x_ref, xall_ref, 0, 4, 0, gsend, grecv)
    ge = [GatherY(eall_ref.at[0, 0], eall_ref, 2 * p, 2, 10 + 10 * p, gsend, grecv) for p in (0, 1)]
    gx.start_first()
    keep = pltpu.make_async_copy(x_ref, xall_ref.at[0, 0], local)
    keep.start()
    ids = [
        remote(gsend, grecv, 30 + n, ids_ref, idall_ref.at[i, slot], peer)
        for n, (peer, i, slot) in enumerate(grid_peers)
    ]
    for copy in ids:
        copy.start()
    idall_ref[0, 0] = ids_ref[...]

    for b in range(4):
        for s in range(SIG):
            xpad[b, s] = x_ref[b, :, s * BLK : (s + 1) * BLK]
        xpad[b, SIG] = jnp.zeros((BLK, BLK), BF16)
    for b in range(4):
        for l in range(xloc.shape[1] // BLK):
            xloc[b * BLK : (b + 1) * BLK, l * BLK : (l + 1) * BLK] = xpad[b, idx_ref[b, l]]

    def split(src):
        def some(k, _):
            k = pl.ds(pl.multiple_of(k * 256, 256), 256)
            both = src[k].astype(F32)
            w[k, :NOCC] = both[:, 0, :].astype(BF16)
            w[k, NOCC:] = both[:, 1, :].astype(BF16)
            return 0

        lax.fori_loop(0, w.shape[0] // 256, some, 0)

    split(occ_ref)
    od[...] = jnp.dot(xloc[...], w[...], preferred_element_type=F32)
    osum = [
        remote(osend, orecv, d - 1, od.at[rows_of(lax.rem(a + d, 8) * 64, 64)], orec.at[d - 1], ao_peers[d - 1])
        for d in range(1, 8)
    ]
    for copy in osum:
        copy.start()

    def densities(dest, store):
        def one(t, _):
            v = dest * 4 + t
            load(v).wait()
            split(buf.at[v])
            store(
                pl.ds(pl.multiple_of(t * 256, 256), 256),
                jnp.dot(xloc[...], w[...], preferred_element_type=F32),
            )
            return 0

        lax.fori_loop(0, 4, one, 0)

    batch = [pl.ds(b * BLK, BLK) for b in range(4)]
    to_opp = [remote(send, recv, b, opp.at[batch[b]], rec1.at[batch[b]], (right, left)[b % 2]) for b in range(4)]
    to_right = [remote(send, recv, 4 + b, part.at[0, batch[b]], rec2.at[0, batch[b]], right) for b in range(4)]
    to_left = [remote(send, recv, 8 + b, part.at[1, batch[b]], rec2.at[1, batch[b]], left) for b in range(4)]
    half = [pl.ds(256 * p, 256) for p in (0, 1)]
    to_pair = [remote(send, recv, 12 + p, zsend.at[half[p]], zrec.at[half[p]], across) for p in (0, 1)]

    def store_opp(cols, value):
        opp[:, cols] = value.astype(BF16)

    def store_side(side):
        def store(cols, value):
            for b in range(4):
                piece = value[b * BLK : (b + 1) * BLK]
                if b % 2 == side:
                    own[batch[b], cols] = piece
                else:
                    part[side, batch[b], cols] = piece.astype(BF16)

        return store

    def store_own(cols, value):
        own[:, cols] = value

    def add(side, b):
        to_opp[b].wait_recv()

        def some(i, _):
            r = rows_of(b * BLK + i * 16, 16)
            part[side, r] = (own[r] + rec1[r].astype(F32)).astype(BF16)
            return 0

        lax.fori_loop(0, BLK // 16, some, 0)

    densities(order[0], store_opp)
    for copy in to_opp:
        copy.start()
    gx.start_second()
    for copy in osum:
        copy.wait_recv()
    mine64 = rows_of(a * 64, 64)
    og[mine64] = (od[mine64] + sum(orec[n] for n in range(7))).astype(BF16)
    ogat = [
        remote(osend, orecv, 7 + d - 1, og.at[mine64], og.at[mine64], ao_peers[d - 1])
        for d in range(1, 8)
    ]
    for copy in ogat:
        copy.start()

    densities(order[1], store_side(0))
    to_right[1].start()
    add(0, 0)
    to_right[0].start()
    to_right[3].start()
    add(0, 2)
    to_right[2].start()
    gx.forward()
    densities(order[2], store_side(1))
    to_left[0].start()
    add(1, 1)
    to_left[1].start()
    to_left[2].start()
    add(1, 3)
    to_left[3].start()
    densities(order[3], store_own)
    gx.spread()

    theirs = pl.ds(pl.multiple_of((1 - zl) * 512, 512), 512)
    mine = pl.ds(pl.multiple_of(zl * 512, 512), 512)

    def total(r, cols):
        return own[r, cols] + rec2[0, r, cols].astype(F32) + rec2[1, r, cols].astype(F32)

    for p in (0, 1):
        for b in (2 * p, 2 * p + 1):
            to_right[b].wait_recv()
            to_left[b].wait_recv()

        def give(i, _):
            r = rows_of(256 * p + i * 16, 16)
            zsend[r] = total(r, theirs).astype(BF16)
            return 0

        lax.fori_loop(0, 16, give, 0)
        to_pair[p].start()
    for copy in ogat:
        copy.wait_recv()
    gx.spread_opposite()

    for p in (0, 1):
        to_pair[p].wait_recv()

        def last(i, _):
            r = rows_of(256 * p + i * 16, 16)
            lg[r] = (total(r, mine) + zrec[r].astype(F32)).astype(BF16)
            return 0

        lax.fori_loop(0, 16, last, 0)
        for b in (2 * p, 2 * p + 1):
            ore = og[batch[b], :NOCC].astype(F32)
            oim = og[batch[b], NOCC:].astype(F32)
            ww = jnp.concatenate(
                [
                    jnp.concatenate([ore, oim], axis=1),
                    jnp.concatenate([-oim, ore], axis=1),
                ],
                axis=0,
            ).astype(BF16)
            both = jnp.concatenate([kern_ref[b], kern_ref[b]], axis=1)
            for v in range(2):
                cols = pl.ds(v * 256, 256)
                rho = lax.dot_general(
                    lg[batch[b], cols], ww, (((1,), (1,)), ((), ())), preferred_element_type=F32
                )
                m = (rho * both).astype(BF16)
                eall_ref[0, 0, b, :, cols] = jnp.dot(m, ww, preferred_element_type=F32).astype(BF16)
        ge[p].start_first()
        ge[p].start_second()

    for p in (0, 1):
        ge[p].forward()
        ge[p].spread()
    for p in (0, 1):
        ge[p].spread_opposite()
    for gather in [gx] + ge:
        gather.finish()
    keep.wait()
    for copy in ids:
        copy.wait()
    for copy in ogat + osum + to_opp + to_right + to_left + to_pair:
        copy.wait_send()


def exchange_step(idx, trial, colloc, occupied, ids, kern):
    rows = trial.shape[0]
    hbm = pl.BlockSpec(memory_space=pl.ANY)
    vmem = pl.BlockSpec(memory_space=pltpu.VMEM)
    return pl.pallas_call(
        main_kernel,
        out_shape=(
            jax.ShapeDtypeStruct((2, 4) + colloc.shape, BF16),
            jax.ShapeDtypeStruct((2, 4, 4, BLK, 512), BF16),
            jax.ShapeDtypeStruct((2, 4) + ids.shape, jnp.int32),
        ),
        in_specs=[pl.BlockSpec(memory_space=pltpu.SMEM), hbm, vmem, vmem, vmem, vmem],
        out_specs=(hbm, vmem, vmem),
        scratch_shapes=[
            pltpu.VMEM((16, rows, 2, NOCC), BF16),
            pltpu.VMEM((rows, 256), BF16),
            pltpu.VMEM((4, SIG + 1, BLK, BLK), BF16),
            pltpu.VMEM((ROWS, rows), BF16),
            pltpu.VMEM((ROWS, 1024), BF16),
            pltpu.VMEM((2, ROWS, 1024), BF16),
            pltpu.VMEM((ROWS, 1024), F32),
            pltpu.VMEM((ROWS, 1024), BF16),
            pltpu.VMEM((2, ROWS, 1024), BF16),
            pltpu.VMEM((ROWS, 512), BF16),
            pltpu.VMEM((ROWS, 512), BF16),
            pltpu.VMEM((ROWS, 512), BF16),
            pltpu.VMEM((ROWS, 2 * NOCC), F32),
            pltpu.VMEM((7, ROWS // 8, 2 * NOCC), F32),
            pltpu.VMEM((ROWS, 2 * NOCC), BF16),
            pltpu.SemaphoreType.DMA((16,)),
            pltpu.SemaphoreType.DMA((14,)),
            pltpu.SemaphoreType.DMA((14,)),
            pltpu.SemaphoreType.DMA((14,)),
            pltpu.SemaphoreType.DMA((14,)),
            pltpu.SemaphoreType.DMA((37,)),
            pltpu.SemaphoreType.DMA((37,)),
            pltpu.SemaphoreType.DMA,
        ],
        compiler_params=pltpu.CompilerParams(
            vmem_limit_bytes=58 << 20, collective_id=0, has_side_effects=True
        ),
        name="exchange_step",
    )(idx, trial, colloc, occupied, ids, kern)


def panel_kernel(ids_ref, base_ref, x_ref, e_ref, out_ref, acc):
    acc[...] = jnp.zeros_like(acc)
    base = base_ref[0]

    def batch(j, _):
        for s in range(SIG):
            r = ids_ref[j, s] - base

            @pl.when((r >= 0) & (r < 6))
            def _():
                acc[jnp.clip(r, 0, 5)] += lax.dot_general(
                    x_ref[j, :, s * BLK : (s + 1) * BLK], e_ref[j], (((0,), (0,)), ((), ())),
                    preferred_element_type=F32,
                )

        return 0

    lax.fori_loop(0, 32, batch, 0)
    out_ref[...] = acc[...].astype(out_ref.dtype)


def panel(ids, base, xall, eall, dtype):
    vmem = pl.BlockSpec(memory_space=pltpu.VMEM)
    smem = pl.BlockSpec(memory_space=pltpu.SMEM)
    return pl.pallas_call(
        panel_kernel,
        out_shape=jax.ShapeDtypeStruct((6, BLK, 512), dtype),
        in_specs=[smem, smem, vmem, vmem],
        out_specs=vmem,
        scratch_shapes=[pltpu.VMEM((6, BLK, 512), F32)],
        compiler_params=pltpu.CompilerParams(vmem_limit_bytes=48 << 20),
        cost_estimate=pl.CostEstimate(flops=10**9, bytes_accessed=20 * 10**6, transcendentals=0),
        name="panel",
    )(ids, base, xall, eall)


def place_of(ids, wanted):
    hit = ids[..., None, :] == wanted[..., :, None]
    where = jnp.arange(SIG, dtype=jnp.int32)
    return SIG + jnp.sum(jnp.where(hit, where - SIG, 0), axis=-1).astype(jnp.int32)


def on_device(trial, occupied, colloc, blocks, coords, weights):
    zh, y, c, x, zl = coords_of()
    nloc = trial.shape[0] // BLK
    local = lax.axis_index("ao") * nloc + jnp.arange(nloc, dtype=jnp.int32)
    differ = coords[:, :, :, None] - coords[:, :, None, :]
    square = jnp.sum(differ * differ, axis=1)
    kern = weights[:, :, None] * weights[:, None, :] / jnp.sqrt(square + 0.25)
    padded = jnp.pad(blocks, ((0, 4), (0, BLK - SIG)))
    xall, eall, idall = exchange_step(
        place_of(blocks, local), trial, colloc, occupied, padded, kern
    )
    ids = idall[:, :, :4, :SIG].reshape(32, SIG)
    xs = xall.reshape(32, BLK, SIG * BLK)
    es = eall.reshape(32, BLK, 512)
    first = (y * 2 + c) * 6
    give = panel(ids, ((1 - zh) * 48 + first)[None].astype(jnp.int32), xs, es, BF16)
    n = lax.axis_size("grid")
    got = lax.ppermute(give, "grid", [(i, (i + n // 2) % n) for i in range(n)])
    keep = panel(ids, (zh * 48 + first)[None].astype(jnp.int32), xs, es, F32)
    total = keep + got.astype(F32)
    return total.reshape(6 * BLK, 2, 2, NOCC).transpose(1, 0, 2, 3)


def solution(mesh):
    in_specs = (
        P("ao", None, None, None),
        P("ao", None, None),
        P("grid", None, None),
        P("grid", None),
        P("grid", None, None),
        P("grid", None),
    )
    out_specs = P("ao", "grid", None, None)
    return jax.shard_map(
        on_device, mesh=mesh, in_specs=in_specs, out_specs=out_specs, check_vma=False
    )
```

time: 804 us -> 135 us (0.17)
  blocking collectives: 344 us -> 0 us
  waiting for transfers between devices: 194 us -> 4.77 us
  Pallas kernels: 0 us -> 107 us
  local copies, waits for them, and re-layouts: 104 us -> 9.88 us
  other arithmetic: 87.8 us -> 4.88 us
  matrix products: 58.2 us -> 0 us
  between operations: 13.4 us -> 0.05 us
    psum x1 -> x0, blocking collectives: 344 us -> none  [on_device(): summed = lax.psum(partial_dens, 'ao')]
    reduce_scatter x1 -> x0, waiting for transfers between devices: 194 us -> none  [on_device(): lax.psum_scatter(panel, 'grid', scatter_dimension=0, tiled=True)]
    pallas_call x0 -> x3, Pallas kernels: none -> 107 us  [the longest x1 83.9 us: exchange_step(): pl.pallas_call(main_kernel, out_shape=(jax.ShapeDtypeStruct((2, 4) + coll...]
    dot_general x40 -> x0, matrix products: 58.2 us -> none  [the longest x4 46.4 us: density(): jnp.dot(values, picked.reshape(SIG * BLK, width + 2 * NOCC), preferred_el...]
    mul x4 -> x0, other arithmetic: 44.2 us -> none  [density(): combined[jnp.clip(local_ids, 0, nblk_local - 1)]]
    gather x4 -> x0, local copies, waits for them, and re-layouts: 43.8 us -> none  [density(): combined[jnp.clip(local_ids, 0, nblk_local - 1)]]
    scatter-add x4 -> x0, other arithmetic: 31.8 us -> none  [add_batch(): return (running.at[block_ids].add(contrib), None)]
    concatenate x2 -> x0, local copies, waits for them, and re-layouts: 23.6 us -> none  [on_device(): jnp.concatenate([trial.reshape(local_rows, width), occupied.reshape(local...]
  transfers between devices with their start and end apart: 1 -> 1, of which waited for: 1 -> 1; matrix products, arithmetic and copies ran while one was open for 0% -> 0% of each run, Pallas kernels for 0% -> 9%
where the time goes in v2:
time: 135 us; the launch traced here: 134 us
  Pallas kernels  107 us (79%)
  local copies, waits for them, and re-layouts  9.88 us (7%)
  starting transfers between devices  6.9 us (5%)
  other arithmetic  4.88 us (4%)
  waiting for transfers between devices  4.77 us (4%)
    pallas_call x1, Pallas kernels, exchange_step(): pl.pallas_call(main_kernel, out_shape=(jax.ShapeDtypeStruct((2, 4) + coll...  83.9 us
    pallas_call x2, Pallas kernels, panel(): pl.pallas_call(panel_kernel, out_shape=jax.ShapeDtypeStruct((6, BLK, 512)...  23.2 us
    ppermute x1, starting transfers between devices, on_device(): got = lax.ppermute(give, 'grid', [(i, (i + n // 2) % n) for i in range(n)])  6.9 us
    unnamed x5, local copies, waits for them, and re-layouts  5.07 us
    ppermute x1, waiting for transfers between devices, on_device(): got = lax.ppermute(give, 'grid', [(i, (i + n // 2) % n) for i in range(n)])  4.77 us
  transfers between devices with their start and end apart: 1, of which 1 were waited for; matrix products, arithmetic and copies ran while one was open for 0% of the time, Pallas kernels for 9%

profile of v2, /device:TPU:6, one launch (start us, length us, event | category | flops | bytes accessed | tf_op | source)
XLA Modules:
  0.0 133.6 jit_solution(7295360813914927498)
XLA Ops:
  0.0 1.3 pad.4.ids_ref
  1.3 1.0 select_reduce_fusion
  2.3 0.1 copy.10
  2.4 0.6 broadcast_add_fusion.idx_ref
  3.0 0.7 copy.11
  3.7 0.3 multiply_reduce_fusion
  3.9 1.6 %rsqrt_multiply_fusion.kern_ref = f32[4,128,128]{2,1,0:T(8,128)} fusion(f32[4,128,128]{2,1,0:T(8,128)S(1)} %multiply_reduce_fusion, f32[4,128]{1,0:T(4,128)} %param.11), kind=kLoop, calls=%fused_computation.3 | loop fusion | flops 196608 | bytes 526336 | tf_op jit(solution)/shard_map/div | solution.py:412
  5.5 83.9 %exchange_step.1 = (bf16[2,4,4,128,1536]{4,3,2,1,0:T(8,128)(2,1)}, bf16[2,4,4,128,512]{4,3,2,1,0:T(8,128)(2,1)}, s32[2,4,8,128]{3,2,1,0:T(8,128)}) custom-call(s32[4,12]{1,0:T(4,128)} %broadcast_add_fusion.idx_ref, bf16[1536,16,2,128]{3,2,1,0:T(2,128)(2,1)} %trial_ref.1, bf16[4,128,1536]{2,1,0:T(8,128)(2,1)} %x_ref.1, bf16[1536,2,128]{2,1,0:T(2,128)(2,1)} %occ_ref.1, ...), custom_call_target="tpu_custom_call" | custom-call | tf_op jit(solution)/shard_map/exchange_step/pallas_call | solution.py:323
  89.5 0.8 slice.3
  90.2 0.0 copy-start
  90.2 2.2 %copy-done = bf16[2,4,4,128,512]{4,3,2,1,0:T(8,128)(2,1)S(1)} copy-done((bf16[2,4,4,128,512]{4,3,2,1,0:T(8,128)(2,1)S(1)}, bf16[2,4,4,128,512]{4,3,2,1,0:T(8,128)(2,1)}, u32[]{:S(2)}) %copy-start) | copy-done | bytes 4194328
  92.4 11.8 %panel.3 = bf16[6,128,512]{2,1,0:T(8,128)(2,1)S(1)} custom-call(s32[32,12]{1,0:T(8,128)S(1)} %bitcast.10, s32[1]{0:T(128)} %bitcast.4.base_ref, bf16[32,128,1536]{2,1,0:T(8,128)(2,1)} %bitcast.12, bf16[32,128,512]{2,1,0:T(8,128)(2,1)S(1)} %bitcast.8), custom_call_target="tpu_custom_call" | custom-call | flops 1000000000 | bytes 20000000 | tf_op jit(solution)/shard_map/panel/pallas_call | solution.py:388
  104.2 6.9 %collective-permute-start = (bf16[6,128,512]{2,1,0:T(8,128)(2,1)S(1)}, bf16[6,128,512]{2,1,0:T(8,128)(2,1)}, u32[]{:S(2)}, u32[]{:S(2)}) collective-permute-start(bf16[6,128,512]{2,1,0:T(8,128)(2,1)S(1)} %panel.3), channel_id=1, source_target_pairs={{0,64},{8,72},{16,80},{24,88},{32,96},{40,104},{48,112},{56,120},{... | collective-permute-start | bytes 2359304 | tf_op jit(solution)/shard_map/ppermute | solution.py:423
  111.1 0.0 copy-start.1
  111.1 2.2 %copy-done.1 = bf16[2,4,4,128,512]{4,3,2,1,0:T(8,128)(2,1)S(1)} copy-done((bf16[2,4,4,128,512]{4,3,2,1,0:T(8,128)(2,1)S(1)}, bf16[2,4,4,128,512]{4,3,2,1,0:T(8,128)(2,1)}, u32[]{:S(2)}) %copy-start.1) | copy-done | bytes 4194328
  113.3 11.4 %panel.2 = f32[6,128,512]{2,1,0:T(8,128)S(1)} custom-call(s32[32,12]{1,0:T(8,128)S(1)} %bitcast.11, s32[1]{0:T(128)} %bitcast.1.base_ref, bf16[32,128,1536]{2,1,0:T(8,128)(2,1)} %bitcast.13, bf16[32,128,512]{2,1,0:T(8,128)(2,1)S(1)} %bitcast.9), custom_call_target="tpu_custom_call" | custom-call | flops 1000000000 | bytes 20000000 | tf_op jit(solution)/shard_map/panel/pallas_call | solution.py:388
  124.7 4.8 %collective-permute-done = bf16[6,128,512]{2,1,0:T(8,128)(2,1)} collective-permute-done((bf16[6,128,512]{2,1,0:T(8,128)(2,1)S(1)}, bf16[6,128,512]{2,1,0:T(8,128)(2,1)}, u32[]{:S(2)}, u32[]{:S(2)}) %collective-permute-start) | collective-permute-done | bytes 786464 | tf_op jit(solution)/shard_map/ppermute | solution.py:423
  129.5 1.4 %convert_add_fusion = f32[6,128,512]{2,1,0:T(8,128)S(1)} fusion(f32[6,128,512]{2,1,0:T(8,128)S(1)} %panel.2, bf16[6,128,512]{2,1,0:T(8,128)(2,1)} %collective-permute-done), kind=kLoop, calls=%fused_computation.1 | loop fusion | flops 786432 | bytes 3932160 | tf_op jit(solution)/shard_map/add | solution.py:425
  130.9 1.0 reshape.24
  131.9 1.7 %copy.15 = f32[768,2,2,128]{3,2,0,1:T(2,128)} copy(f32[768,2,2,128]{3,2,1,0:T(2,128)S(1)} %reshape.24) | data formatting | bytes 3145728 | tf_op jit(solution)/shard_map/reshape | solution.py:426
  (1 shorter events, 0.0 us)
Async XLA Ops:
  90.2 2.2 %copy-start = (bf16[2,4,4,128,512]{4,3,2,1,0:T(8,128)(2,1)S(1)}, bf16[2,4,4,128,512]{4,3,2,1,0:T(8,128)(2,1)}, u32[]{:S(2)}) copy-start(bf16[2,4,4,128,512]{4,3,2,1,0:T(8,128)(2,1)} %get-tuple-element.10) | copy-start | bytes 12582916
  104.2 25.3 %collective-permute-start = (bf16[6,128,512]{2,1,0:T(8,128)(2,1)S(1)}, bf16[6,128,512]{2,1,0:T(8,128)(2,1)}, u32[]{:S(2)}, u32[]{:S(2)}) collective-permute-start(bf16[6,128,512]{2,1,0:T(8,128)(2,1)S(1)} %panel.3), channel_id=1, source_target_pairs={{0,64},{8,72},{16,80},{24,88},{32,96},{40,104},{48,112},{56,120},{... | collective-permute-start | bytes 2359304 | tf_op jit(solution)/shard_map/ppermute | solution.py:423
  111.1 2.2 %copy-start.1 = (bf16[2,4,4,128,512]{4,3,2,1,0:T(8,128)(2,1)S(1)}, bf16[2,4,4,128,512]{4,3,2,1,0:T(8,128)(2,1)}, u32[]{:S(2)}) copy-start(bf16[2,4,4,128,512]{4,3,2,1,0:T(8,128)(2,1)} %get-tuple-element.10) | copy-start | bytes 12582916

commit v3 on v2

--- a/solution.py
+++ b/solution.py
@@ -26,9 +26,9 @@
 
 
 class GatherY:
-    def __init__(self, own, slots, first, count, base, send, recv):
+    def __init__(self, own, slots, first, count, base, send, recv, tail=()):
         self.own, self.slots, self.base = own, slots, base
-        self.send, self.recv = send, recv
+        self.send, self.recv, self.tail = send, recv, tail
         half = count // 2
         self.every = pl.ds(first, count)
         self.lo, self.hi = pl.ds(first, half), pl.ds(first + half, half)
@@ -38,18 +38,25 @@
         self.twin = device_at(zh, y, 1 - c, x, zl)
 
     def at(self, n):
-        s, own, lo, hi, every = self.slots, self.own, self.lo, self.hi, self.every
+        own, slots, lo, hi, every = self.own, self.slots, self.lo, self.hi, self.every
+
+        def o(b):
+            return own.at[(b,) + self.tail]
+
+        def s(i, slot, b):
+            return slots(i, slot).at[(b,) + self.tail]
+
         src, dst, to = [
-            (own.at[lo], s.at[0, 1, lo], self.right),
-            (own.at[hi], s.at[0, 2, hi], self.left),
-            (own.at[hi], s.at[0, 1, hi], self.right),
-            (own.at[lo], s.at[0, 2, lo], self.left),
-            (own.at[every], s.at[1, 0, every], self.twin),
-            (s.at[0, 1, lo], s.at[0, 3, lo], self.right),
-            (s.at[0, 2, hi], s.at[0, 3, hi], self.left),
-            (s.at[0, 1, every], s.at[1, 1, every], self.twin),
-            (s.at[0, 2, every], s.at[1, 2, every], self.twin),
-            (s.at[0, 3, every], s.at[1, 3, every], self.twin),
+            (o(lo), s(0, 1, lo), self.right),
+            (o(hi), s(0, 2, hi), self.left),
+            (o(hi), s(0, 1, hi), self.right),
+            (o(lo), s(0, 2, lo), self.left),
+            (o(every), s(1, 0, every), self.twin),
+            (s(0, 1, lo), s(0, 3, lo), self.right),
+            (s(0, 2, hi), s(0, 3, hi), self.left),
+            (s(0, 1, every), s(1, 1, every), self.twin),
+            (s(0, 2, every), s(1, 2, every), self.twin),
+            (s(0, 3, every), s(1, 3, every), self.twin),
         ][n]
         return remote(self.send, self.recv, self.base + n, src, dst, to)
 
@@ -76,9 +83,11 @@
             self.at(n).wait_recv()
         self.at(9).start()
 
-    def finish(self):
-        for n in (4, 7, 8, 9):
+    def arrived(self, *which):
+        for n in which:
             self.at(n).wait_recv()
+
+    def sent(self):
         for n in range(10):
             self.at(n).wait_send()
 
@@ -102,13 +111,14 @@
 
 
 def main_kernel(
-    idx_ref, trial_ref, x_ref, occ_ref, ids_ref, kern_ref,
-    xall_ref, eall_ref, idall_ref,
-    buf, w, xpad, xloc, opp, part, own, rec1, rec2, zsend, zrec, lg, od, orec, og,
-    load_sem, send, recv, osend, orecv, gsend, grecv, local,
+    inv_ref, trial_ref, x_ref, occ_ref, place_ref, coords_ref, weights_ref, out_ref,
+    x00, x01, x02, x03, x10, x11, x12, x13, eall, places, table, kern, acc, give, got,
+    buf, w, xloc, opp, part, own, rec1, rec2, zsend, zrec, lg, od, orec, og,
+    load_sem, send, recv, osend, orecv, gsend, grecv, hsend, hrecv, local,
 ):
     zh, y, c, x, zl = coords_of()
     a = x * 2 + zl
+    beyond = device_at(1 - zh, y, c, x, zl)
     right = device_at(zh, y, c, lax.rem(x + 1, 4), zl)
     left = device_at(zh, y, c, lax.rem(x + 3, 4), zl)
     across = device_at(zh, y, c, x, 1 - zl)
@@ -128,28 +138,34 @@
         for same in (True, False)
         if d or not same
     ]
-    greet(ao_peers + [peer for peer, _, _ in grid_peers])
-
-    gx = GatherY(x_ref, xall_ref, 0, 4, 0, gsend, grecv)
-    ge = [GatherY(eall_ref.at[0, 0], eall_ref, 2 * p, 2, 10 + 10 * p, gsend, grecv) for p in (0, 1)]
+    greet(ao_peers + [peer for peer, _, _ in grid_peers] + [beyond])
+
+    for b in range(4):
+        for n in range(SIG):
+            x00[b, n] = x_ref[b, :, n * BLK : (n + 1) * BLK]
+    xs = [[x00, x01, x02, x03], [x10, x11, x12, x13]]
+    gx = GatherY(x00, lambda i, slot: xs[i][slot], 0, 4, 0, gsend, grecv, (pl.ds(0, SIG),))
+    ge = [
+        GatherY(eall.at[0, 0], lambda i, slot: eall.at[i, slot], 2 * p, 2, 10 + 10 * p, gsend, grecv)
+        for p in (0, 1)
+    ]
     gx.start_first()
-    keep = pltpu.make_async_copy(x_ref, xall_ref.at[0, 0], local)
-    keep.start()
-    ids = [
-        remote(gsend, grecv, 30 + n, ids_ref, idall_ref.at[i, slot], peer)
+    tables = [
+        remote(gsend, grecv, 30 + n, place_ref, places.at[i, slot], peer)
         for n, (peer, i, slot) in enumerate(grid_peers)
     ]
-    for copy in ids:
+    for copy in tables:
         copy.start()
-    idall_ref[0, 0] = ids_ref[...]
-
-    for b in range(4):
-        for s in range(SIG):
-            xpad[b, s] = x_ref[b, :, s * BLK : (s + 1) * BLK]
-        xpad[b, SIG] = jnp.zeros((BLK, BLK), BF16)
+    places[0, 0] = place_ref[...]
+    for i in range(2):
+        for slot in range(4):
+            for b in range(4):
+                xs[i][slot][b, SIG] = jnp.zeros((BLK, BLK), BF16)
     for b in range(4):
         for l in range(xloc.shape[1] // BLK):
-            xloc[b * BLK : (b + 1) * BLK, l * BLK : (l + 1) * BLK] = xpad[b, idx_ref[b, l]]
+            xloc[b * BLK : (b + 1) * BLK, l * BLK : (l + 1) * BLK] = x00[
+                b, inv_ref[b, a * (xloc.shape[1] // BLK) + l]
+            ]
 
     def split(src):
         def some(k, _):
@@ -250,6 +266,24 @@
     densities(order[3], store_own)
     gx.spread()
 
+    def spread_row(row):
+        return jnp.broadcast_to(row, (BLK, BLK))
+
+    for b in range(4):
+        square = None
+        for k in range(3):
+            along = spread_row(coords_ref[k, b : b + 1, :])
+            differ = along.T - along
+            square = differ * differ if square is None else square + differ * differ
+        quad = spread_row(weights_ref[b : b + 1, :])
+        kern[b] = quad.T * quad / jnp.sqrt(square + 0.25)
+    for copy in tables:
+        copy.wait_recv()
+    fill = pltpu.make_async_copy(places, table, local)
+    fill.start()
+    fill.wait()
+    acc[...] = jnp.zeros_like(acc)
+
     theirs = pl.ds(pl.multiple_of((1 - zl) * 512, 512), 512)
     mine = pl.ds(pl.multiple_of(zl * 512, 512), 512)
 
@@ -261,12 +295,12 @@
             to_right[b].wait_recv()
             to_left[b].wait_recv()
 
-        def give(i, _):
+        def hand(i, _):
             r = rows_of(256 * p + i * 16, 16)
             zsend[r] = total(r, theirs).astype(BF16)
             return 0
 
-        lax.fori_loop(0, 16, give, 0)
+        lax.fori_loop(0, 16, hand, 0)
         to_pair[p].start()
     for copy in ogat:
         copy.wait_recv()
@@ -291,48 +325,93 @@
                 ],
                 axis=0,
             ).astype(BF16)
-            both = jnp.concatenate([kern_ref[b], kern_ref[b]], axis=1)
+            both = jnp.concatenate([kern[b], kern[b]], axis=1)
             for v in range(2):
                 cols = pl.ds(v * 256, 256)
                 rho = lax.dot_general(
                     lg[batch[b], cols], ww, (((1,), (1,)), ((), ())), preferred_element_type=F32
                 )
                 m = (rho * both).astype(BF16)
-                eall_ref[0, 0, b, :, cols] = jnp.dot(m, ww, preferred_element_type=F32).astype(BF16)
+                eall[0, 0, b, :, cols] = jnp.dot(m, ww, preferred_element_type=F32).astype(BF16)
         ge[p].start_first()
         ge[p].start_second()
 
-    for p in (0, 1):
-        ge[p].forward()
-        ge[p].spread()
-    for p in (0, 1):
-        ge[p].spread_opposite()
+    first = (y * 2 + c) * 6
+
+    def panel(i, slot, start, stop):
+        def row(r, _):
+            block = jnp.where(r < 6, (1 - zh) * 48 + first + r, zh * 48 + first + r - 6)
+            tiles = [xs[i][slot][b, table[i, slot, b, block]] for b in range(4)]
+            acc[r] += lax.dot_general(
+                jnp.concatenate(tiles, axis=0), eall[i, slot].reshape(4 * BLK, 512),
+                (((0,), (0,)), ((), ())), preferred_element_type=F32,
+            )
+            return 0
+
+        lax.fori_loop(start, stop, row, 0)
+
+    ge[0].forward()
+    ge[0].spread()
+    panel(0, 0, 0, 12)
+    ge[1].forward()
+    ge[1].spread()
     for gather in [gx] + ge:
-        gather.finish()
-    keep.wait()
-    for copy in ids:
-        copy.wait()
-    for copy in ogat + osum + to_opp + to_right + to_left + to_pair:
+        gather.arrived(4)
+    panel(1, 0, 0, 12)
+    panel(0, 1, 0, 12)
+    panel(0, 2, 0, 12)
+    ge[0].spread_opposite()
+    ge[1].spread_opposite()
+    for gather in [gx] + ge:
+        gather.arrived(7, 8)
+    panel(1, 1, 0, 12)
+    panel(1, 2, 0, 12)
+    panel(0, 3, 0, 12)
+    for gather in [gx] + ge:
+        gather.arrived(9)
+    over = [remote(hsend, hrecv, n, give.at[n], got.at[n], beyond) for n in range(2)]
+    for n in (0, 1):
+        panel(1, 3, 3 * n, 3 * n + 3)
+        for r in range(3 * n, 3 * n + 3):
+            give[n, r - 3 * n] = acc[r].astype(BF16)
+        over[n].start()
+    panel(1, 3, 6, 12)
+    for r in range(6):
+        if r % 3 == 0:
+            over[r // 3].wait_recv()
+        for v in range(2):
+            for k in range(2):
+                cols = slice(v * 256 + k * 128, v * 256 + k * 128 + 128)
+                out_ref[v, r * BLK : (r + 1) * BLK, k, :] = acc[6 + r, :, cols] + got[
+                    r // 3, r % 3, :, cols
+                ].astype(F32)
+    for gather in [gx] + ge:
+        gather.sent()
+    for copy in tables + over + ogat + osum + to_opp + to_right + to_left + to_pair:
         copy.wait_send()
 
 
-def exchange_step(idx, trial, colloc, occupied, ids, kern):
+def exchange_step(inv, trial, colloc, occupied, coords, weights):
     rows = trial.shape[0]
     hbm = pl.BlockSpec(memory_space=pl.ANY)
     vmem = pl.BlockSpec(memory_space=pltpu.VMEM)
+    smem = pl.BlockSpec(memory_space=pltpu.SMEM)
     return pl.pallas_call(
         main_kernel,
-        out_shape=(
-            jax.ShapeDtypeStruct((2, 4) + colloc.shape, BF16),
-            jax.ShapeDtypeStruct((2, 4, 4, BLK, 512), BF16),
-            jax.ShapeDtypeStruct((2, 4) + ids.shape, jnp.int32),
-        ),
-        in_specs=[pl.BlockSpec(memory_space=pltpu.SMEM), hbm, vmem, vmem, vmem, vmem],
-        out_specs=(hbm, vmem, vmem),
+        out_shape=jax.ShapeDtypeStruct((2, 6 * BLK, 2, NOCC), F32),
+        in_specs=[smem, hbm, vmem, vmem, vmem, vmem, vmem],
+        out_specs=vmem,
         scratch_shapes=[
+            *[pltpu.VMEM((4, SIG + 1, BLK, BLK), BF16)] * 8,
+            pltpu.VMEM((2, 4, 4, BLK, 512), BF16),
+            pltpu.VMEM((2, 4) + inv.shape, jnp.int32),
+            pltpu.SMEM((2, 4) + inv.shape, jnp.int32),
+            pltpu.VMEM((4, BLK, BLK), F32),
+            pltpu.VMEM((12, BLK, 512), F32),
+            pltpu.VMEM((2, 3, BLK, 512), BF16),
+            pltpu.VMEM((2, 3, BLK, 512), BF16),
             pltpu.VMEM((16, rows, 2, NOCC), BF16),
             pltpu.VMEM((rows, 256), BF16),
-            pltpu.VMEM((4, SIG + 1, BLK, BLK), BF16),
             pltpu.VMEM((ROWS, rows), BF16),
             pltpu.VMEM((ROWS, 1024), BF16),
             pltpu.VMEM((2, ROWS, 1024), BF16),
@@ -352,49 +431,15 @@
             pltpu.SemaphoreType.DMA((14,)),
             pltpu.SemaphoreType.DMA((37,)),
             pltpu.SemaphoreType.DMA((37,)),
+            pltpu.SemaphoreType.DMA((2,)),
+            pltpu.SemaphoreType.DMA((2,)),
             pltpu.SemaphoreType.DMA,
         ],
         compiler_params=pltpu.CompilerParams(
-            vmem_limit_bytes=58 << 20, collective_id=0, has_side_effects=True
+            vmem_limit_bytes=63 << 20, collective_id=0, has_side_effects=True
         ),
         name="exchange_step",
-    )(idx, trial, colloc, occupied, ids, kern)
-
-
-def panel_kernel(ids_ref, base_ref, x_ref, e_ref, out_ref, acc):
-    acc[...] = jnp.zeros_like(acc)
-    base = base_ref[0]
-
-    def batch(j, _):
-        for s in range(SIG):
-            r = ids_ref[j, s] - base
-
-            @pl.when((r >= 0) & (r < 6))
-            def _():
-                acc[jnp.clip(r, 0, 5)] += lax.dot_general(
-                    x_ref[j, :, s * BLK : (s + 1) * BLK], e_ref[j], (((0,), (0,)), ((), ())),
-                    preferred_element_type=F32,
-                )
-
-        return 0
-
-    lax.fori_loop(0, 32, batch, 0)
-    out_ref[...] = acc[...].astype(out_ref.dtype)
-
-
-def panel(ids, base, xall, eall, dtype):
-    vmem = pl.BlockSpec(memory_space=pltpu.VMEM)
-    smem = pl.BlockSpec(memory_space=pltpu.SMEM)
-    return pl.pallas_call(
-        panel_kernel,
-        out_shape=jax.ShapeDtypeStruct((6, BLK, 512), dtype),
-        in_specs=[smem, smem, vmem, vmem],
-        out_specs=vmem,
-        scratch_shapes=[pltpu.VMEM((6, BLK, 512), F32)],
-        compiler_params=pltpu.CompilerParams(vmem_limit_bytes=48 << 20),
-        cost_estimate=pl.CostEstimate(flops=10**9, bytes_accessed=20 * 10**6, transcendentals=0),
-        name="panel",
-    )(ids, base, xall, eall)
+    )(inv, trial, colloc, occupied, inv, coords, weights)
 
 
 def place_of(ids, wanted):
@@ -404,26 +449,10 @@
 
 
 def on_device(trial, occupied, colloc, blocks, coords, weights):
-    zh, y, c, x, zl = coords_of()
-    nloc = trial.shape[0] // BLK
-    local = lax.axis_index("ao") * nloc + jnp.arange(nloc, dtype=jnp.int32)
-    differ = coords[:, :, :, None] - coords[:, :, None, :]
-    square = jnp.sum(differ * differ, axis=1)
-    kern = weights[:, :, None] * weights[:, None, :] / jnp.sqrt(square + 0.25)
-    padded = jnp.pad(blocks, ((0, 4), (0, BLK - SIG)))
-    xall, eall, idall = exchange_step(
-        place_of(blocks, local), trial, colloc, occupied, padded, kern
-    )
-    ids = idall[:, :, :4, :SIG].reshape(32, SIG)
-    xs = xall.reshape(32, BLK, SIG * BLK)
-    es = eall.reshape(32, BLK, 512)
-    first = (y * 2 + c) * 6
-    give = panel(ids, ((1 - zh) * 48 + first)[None].astype(jnp.int32), xs, es, BF16)
-    n = lax.axis_size("grid")
-    got = lax.ppermute(give, "grid", [(i, (i + n // 2) % n) for i in range(n)])
-    keep = panel(ids, (zh * 48 + first)[None].astype(jnp.int32), xs, es, F32)
-    total = keep + got.astype(F32)
-    return total.reshape(6 * BLK, 2, 2, NOCC).transpose(1, 0, 2, 3)
+    nblk = trial.shape[0] // BLK * lax.axis_size("ao")
+    inv = place_of(blocks, jnp.arange(nblk, dtype=jnp.int32))
+    inv = jnp.pad(inv, ((0, 4), (0, BLK - nblk)))
+    return exchange_step(inv, trial, colloc, occupied, coords.transpose(1, 0, 2), weights)
 
 
 def solution(mesh):

time: 135 us -> 121 us (0.90)
  Pallas kernels: 107 us -> 115 us
  starting transfers between devices: 6.9 us -> 0 us
  local copies, waits for them, and re-layouts: 9.88 us -> 4.02 us
  other arithmetic: 4.88 us -> 0.11 us
  waiting for transfers between devices: 4.77 us -> 0 us
    pallas_call x3 -> x1, Pallas kernels: 107 us -> 115 us  [exchange_step(): pl.pallas_call(main_kernel, out_shape=jax.ShapeDtypeStruct((2, 6 * BLK, 2...]
    ppermute x1 -> x0, starting transfers between devices: 6.9 us -> none  [on_device(): got = lax.ppermute(give, 'grid', [(i, (i + n // 2) % n) for i in range(n)])]
    ppermute x1 -> x0, waiting for transfers between devices: 4.77 us -> none  [on_device(): got = lax.ppermute(give, 'grid', [(i, (i + n // 2) % n) for i in range(n)])]
    reshape x2 -> x0, local copies, waits for them, and re-layouts: 2.7 us -> none  [on_device(): return total.reshape(6 * BLK, 2, 2, NOCC).transpose(1, 0, 2, 3)]
    unnamed x5 -> x2, local copies, waits for them, and re-layouts: 5.07 us -> 3.42 us
    div x1 -> x0, other arithmetic: 1.6 us -> none  [on_device(): kern = weights[:, :, None] * weights[:, None, :] / jnp.sqrt(square + 0.25)]
    add x1 -> x0, other arithmetic: 1.41 us -> none  [on_device(): total = keep + got.astype(F32)]
  transfers between devices with their start and end apart: 1 -> 0, of which waited for: 1 -> 0; matrix products, arithmetic and copies ran while one was open for 0% -> 0% of each run, Pallas kernels for 9% -> 0%
where the time goes in v3:
time: 121 us; the launch traced here: 119 us
  Pallas kernels  115 us (95%)
  local copies, waits for them, and re-layouts  4.02 us (3%)
    pallas_call x1, Pallas kernels, exchange_step(): pl.pallas_call(main_kernel, out_shape=jax.ShapeDtypeStruct((2, 6 * BLK, 2...  115 us
    unnamed x2, local copies, waits for them, and re-layouts  3.42 us

profile of v3, /device:TPU:6, one launch (start us, length us, event | category | flops | bytes accessed | tf_op | source)
XLA Modules:
  0.0 118.9 jit_solution(17627022826586430409)
XLA Ops:
  0.0 0.8 copy.7
  0.8 0.1 select_reduce_fusion
  0.9 0.6 pad.4.inv_ref.place_ref
  1.5 114.8 %exchange_step.1 = f32[2,768,2,128]{3,2,1,0:T(2,128)} custom-call(s32[8,128]{1,0:T(8,128)} %pad.4.inv_ref.place_ref, bf16[1536,16,2,128]{3,2,1,0:T(2,128)(2,1)} %trial_ref.1, bf16[4,128,1536]{2,1,0:T(8,128)(2,1)} %x_ref.1, bf16[1536,2,128]{2,1,0:T(2,128)(2,1)} %occ_ref.1, s32[8,128]{1,0:T(8,128)} %pad.4.inv_ref.place_ref, f32[3,4,128]{2,1,0:T(4,128)} %bitcast.1, ...), custom_call_target="tpu_custom_call" | custom-call | tf_op jit(solution)/shard_map/exchange_step/pallas_call | solution.py:399
  116.3 2.7 %copy.9 = f32[2,768,2,128]{3,2,1,0:T(2,128)} copy(f32[2,768,2,128]{3,2,1,0:T(2,128)} %exchange_step.1) | data formatting | bytes 3145728
  (2 shorter events, 0.0 us)

commit v4 on v3

v4 whole, which is shorter than its diff:
```python
import functools
import jax
import jax.numpy as jnp
from jax import lax
from jax.experimental import pallas as pl
from jax.experimental.pallas import tpu as pltpu
from jax.sharding import PartitionSpec as P

BLK = 128
NOCC = 128
SIG = 12
F32 = jnp.float32
BF16 = jnp.bfloat16
MESH = pl.DeviceIdType.MESH
ROWS = 512


def coords_of():
    g = lax.axis_index("grid")
    a = lax.axis_index("ao")
    return g // 8, lax.rem(g // 2, 4), lax.rem(g, 2), a // 2, lax.rem(a, 2)


def device_at(zh, y, c, x, zl):
    return (zh * 8 + y * 2 + c, x * 2 + zl)


class GatherY:
    def __init__(self, own, slots, first, count, base, send, recv, tail=()):
        self.own, self.slots, self.base = own, slots, base
        self.send, self.recv, self.tail = send, recv, tail
        half = count // 2
        self.every = pl.ds(first, count)
        self.lo, self.hi = pl.ds(first, half), pl.ds(first + half, half)
        zh, y, c, x, zl = coords_of()
        self.right = device_at(zh, lax.rem(y + 1, 4), c, x, zl)
        self.left = device_at(zh, lax.rem(y + 3, 4), c, x, zl)
        self.twin = device_at(zh, y, 1 - c, x, zl)

    def at(self, n):
        own, slots, lo, hi, every = self.own, self.slots, self.lo, self.hi, self.every

        def o(b):
            return own.at[(b,) + self.tail]

        def s(i, slot, b):
            return slots(i, slot).at[(b,) + self.tail]

        src, dst, to = [
            (o(lo), s(0, 1, lo), self.right),
            (o(hi), s(0, 2, hi), self.left),
            (o(hi), s(0, 1, hi), self.right),
            (o(lo), s(0, 2, lo), self.left),
            (o(every), s(1, 0, every), self.twin),
            (s(0, 1, lo), s(0, 3, lo), self.right),
            (s(0, 2, hi), s(0, 3, hi), self.left),
            (s(0, 1, every), s(1, 1, every), self.twin),
            (s(0, 2, every), s(1, 2, every), self.twin),
            (s(0, 3, every), s(1, 3, every), self.twin),
        ][n]
        return remote(self.send, self.recv, self.base + n, src, dst, to)

    def start_first(self):
        for n in (0, 1):
            self.at(n).start()

    def start_second(self):
        for n in (2, 3, 4):
            self.at(n).start()

    def forward(self):
        for n in (0, 1):
            self.at(n).wait_recv()
            self.at(n + 5).start()

    def spread(self):
        for n in (2, 3):
            self.at(n).wait_recv()
            self.at(n + 5).start()

    def spread_opposite(self):
        for n in (5, 6):
            self.at(n).wait_recv()
        self.at(9).start()

    def arrived(self, *which):
        for n in which:
            self.at(n).wait_recv()

    def sent(self):
        for n in range(10):
            self.at(n).wait_send()


def remote(send, recv, n, src, dst, to):
    return pltpu.make_async_remote_copy(
        src_ref=src, dst_ref=dst, send_sem=send.at[n], recv_sem=recv.at[n],
        device_id=to, device_id_type=MESH,
    )


def greet(peers):
    barrier = pltpu.get_barrier_semaphore()
    for peer in peers:
        pl.semaphore_signal(barrier, inc=1, device_id=peer, device_id_type=MESH)
    pl.semaphore_wait(barrier, len(peers))


def rows_of(start, size):
    return pl.ds(pl.multiple_of(start, size), size)


def main_kernel(
    inv_ref, trial_ref, x_ref, occ_ref, place_ref, coords_ref, weights_ref, out_ref,
    x00, x01, x02, x03, x10, x11, x12, x13, xpad, e0, e1, places, table, kern, acc, give, got,
    buf, w, xloc, opp, part, own, rec1, rec2, zsend, zrec, lg, od, orec, og,
    load_sem, send, recv, osend, orecv, gsend, grecv, hsend, hrecv, local,
):
    zh, y, c, x, zl = coords_of()
    a = x * 2 + zl
    beyond = device_at(1 - zh, y, c, x, zl)
    right = device_at(zh, y, c, lax.rem(x + 1, 4), zl)
    left = device_at(zh, y, c, lax.rem(x + 3, 4), zl)
    across = device_at(zh, y, c, x, 1 - zl)
    order = [lax.rem(x + d, 4) for d in (2, 1, 3, 0)]

    def load(v):
        return pltpu.make_async_copy(trial_ref.at[:, v], buf.at[v], load_sem.at[v])

    for q in (0, 1):
        for dest in order:
            for t in range(2):
                load(dest * 4 + 2 * t + q).start()

    ao_peers = [(lax.axis_index("grid"), lax.rem(a + d, 8)) for d in range(1, 8)]
    grid_peers = [
        (device_at(zh, lax.rem(y + d, 4), c if same else 1 - c, x, zl), 0 if same else 1, slot)
        for d, slot in ((0, 0), (1, 1), (3, 2), (2, 3))
        for same in (True, False)
        if d or not same
    ]
    greet(ao_peers + [peer for peer, _, _ in grid_peers] + [beyond])

    def split(src):
        def some(k, _):
            k = pl.ds(pl.multiple_of(k * 256, 256), 256)
            both = src[k].astype(F32)
            w[k, :NOCC] = both[:, 0, :].astype(BF16)
            w[k, NOCC:] = both[:, 1, :].astype(BF16)
            return 0

        lax.fori_loop(0, w.shape[0] // 256, some, 0)

    zero = jnp.zeros((BLK, BLK), BF16)
    for b in range(4):
        for n in range(SIG):
            xpad[b, n] = x_ref[b, :, n * BLK : (n + 1) * BLK]
        xpad[b, SIG] = zero
    nloc = xloc.shape[1] // BLK
    for b in range(4):
        for l in range(nloc):
            xloc[b * BLK : (b + 1) * BLK, l * BLK : (l + 1) * BLK] = xpad[b, inv_ref[b, a * nloc + l]]

    split(occ_ref)
    od[...] = jnp.dot(xloc[...], w[...], preferred_element_type=F32)
    osum = [
        remote(osend, orecv, d - 1, od.at[rows_of(lax.rem(a + d, 8) * 64, 64)], orec.at[d - 1], ao_peers[d - 1])
        for d in range(1, 8)
    ]
    for copy in osum:
        copy.start()

    for b in range(4):
        for n in range(SIG):
            x00[b, n] = x_ref[b, :, n * BLK : (n + 1) * BLK].T
    xs = [[x00, x01, x02, x03], [x10, x11, x12, x13]]
    es = [e0, e1]
    gx = GatherY(x00, lambda i, slot: xs[i][slot], 0, 4, 0, gsend, grecv, (pl.ds(0, SIG),))
    ge = [
        GatherY(es[q].at[0, 0], lambda i, slot, q=q: es[q].at[i, slot], 0, 4, 10 + 10 * q, gsend, grecv)
        for q in (0, 1)
    ]
    gx.start_first()
    tables = [
        remote(gsend, grecv, 30 + n, place_ref, places.at[i, slot], peer)
        for n, (peer, i, slot) in enumerate(grid_peers)
    ]
    for copy in tables:
        copy.start()
    places[0, 0] = place_ref[...]
    for i in range(2):
        for slot in range(4):
            for b in range(4):
                xs[i][slot][b, SIG] = zero

    def densities(dest, q, store):
        def one(t, _):
            v = dest * 4 + 2 * t + q
            load(v).wait()
            split(buf.at[v])
            store(
                pl.ds(pl.multiple_of(t * 256, 256), 256),
                jnp.dot(xloc[...], w[...], preferred_element_type=F32),
            )
            return 0

        lax.fori_loop(0, 2, one, 0)

    lo, hi = pl.ds(0, 256), pl.ds(256, 256)
    halves = (lo, hi)
    sides = (right, left)
    to_opp = [
        [remote(send, recv, 2 * q + k, opp.at[q, halves[k]], rec1.at[q, halves[k]], sides[k]) for k in (0, 1)]
        for q in (0, 1)
    ]
    to_side = [
        [
            [
                remote(send, recv, 4 + 4 * q + 2 * k + h, part.at[k, q, halves[h]], rec2.at[k, q, halves[h]], sides[k])
                for h in (0, 1)
            ]
            for k in (0, 1)
        ]
        for q in (0, 1)
    ]
    to_pair = [remote(send, recv, 12 + q, zsend.at[q], zrec.at[q], across) for q in (0, 1)]

    def dens_opp(q):
        def store(cols, value):
            opp[q, :, cols] = value.astype(BF16)

        densities(order[0], q, store)
        for copy in to_opp[q]:
            copy.start()

    def dens_side(k, q):
        def store(cols, value):
            own[q, halves[k], cols] = value[256 * k : 256 * k + 256]
            part[k, q, halves[1 - k], cols] = value[256 - 256 * k : 512 - 256 * k].astype(BF16)

        densities(order[1 + k], q, store)
        to_side[q][k][1 - k].start()

    def add_side(k, q):
        to_opp[q][k].wait_recv()

        def some(i, _):
            r = rows_of(256 * k + i * 16, 16)
            part[k, q, r] = (own[q, r] + rec1[q, r].astype(F32)).astype(BF16)
            return 0

        lax.fori_loop(0, 16, some, 0)
        to_side[q][k][k].start()

    def dens_own(q):
        def store(cols, value):
            own[q, :, cols] = value

        densities(order[3], q, store)

    theirs = pl.ds(pl.multiple_of((1 - zl) * 256, 256), 256)
    mine = pl.ds(pl.multiple_of(zl * 256, 256), 256)

    def total(q, r, cols):
        return own[q, r, cols] + rec2[0, q, r, cols].astype(F32) + rec2[1, q, r, cols].astype(F32)

    def to_z(q):
        for k in (0, 1):
            for h in (0, 1):
                to_side[q][k][h].wait_recv()

        def some(i, _):
            r = rows_of(i * 32, 32)
            zsend[q, r] = total(q, r, theirs).astype(BF16)
            return 0

        lax.fori_loop(0, 16, some, 0)
        to_pair[q].start()

    def pair(q):
        to_pair[q].wait_recv()

        def some(i, _):
            r = rows_of(i * 32, 32)
            lg[r] = (total(q, r, mine) + zrec[q, r].astype(F32)).astype(BF16)
            return 0

        lax.fori_loop(0, 16, some, 0)
        for b in range(4):
            rows = pl.ds(b * BLK, BLK)
            ore = og[rows, :NOCC].astype(F32)
            oim = og[rows, NOCC:].astype(F32)
            ww = jnp.concatenate(
                [
                    jnp.concatenate([ore, oim], axis=1),
                    jnp.concatenate([-oim, ore], axis=1),
                ],
                axis=0,
            ).astype(BF16)
            rho = lax.dot_general(
                lg[rows], ww, (((1,), (1,)), ((), ())), preferred_element_type=F32
            )
            m = (rho * jnp.concatenate([kern[b], kern[b]], axis=1)).astype(BF16)
            es[q][0, 0, b] = jnp.dot(m, ww, preferred_element_type=F32).astype(BF16)
        ge[q].start_first()
        ge[q].start_second()

    first = (y * 2 + c) * 6
    GROUP = 3

    def panel(i, slot, q, start, stop, fresh=False):
        def row(n, _):
            lines = []
            for k in range(GROUP):
                r = n * GROUP + k
                block = jnp.where(r < 6, (1 - zh) * 48 + first + r, zh * 48 + first + r - 6)
                lines.append(
                    jnp.concatenate([xs[i][slot][b, table[i, slot, b, block]] for b in range(4)], axis=1)
                )
            value = jnp.dot(
                jnp.concatenate(lines, axis=0), es[q][i, slot].reshape(4 * BLK, 256),
                preferred_element_type=F32,
            ).reshape(GROUP, BLK, 256)
            at = pl.ds(n * GROUP, GROUP)
            acc[q, at] = value if fresh else acc[q, at] + value
            return 0

        lax.fori_loop(start, stop, row, 0)

    over = [
        [remote(hsend, hrecv, 2 * q + n, give.at[q, n], got.at[q, n], beyond) for n in range(2)]
        for q in (0, 1)
    ]

    def middle(q):
        ge[q].spread_opposite()
        ge[q].arrived(4)
        panel(1, 0, q, 0, 4)
        panel(0, 1, q, 0, 4)
        panel(0, 2, q, 0, 4)
        ge[q].arrived(7, 8)
        panel(1, 1, q, 0, 4)
        panel(1, 2, q, 0, 4)
        panel(0, 3, q, 0, 4)

    def last(q):
        ge[q].arrived(9)
        for n in (0, 1):
            panel(1, 3, q, n, n + 1)
            give[q, n] = acc[q, 3 * n : 3 * n + 3].astype(BF16)
            over[q][n].start()
        panel(1, 3, q, 2, 4)

    def finish(q):
        for r in range(6):
            if r % 3 == 0:
                over[q][r // 3].wait_recv()
            for k in range(2):
                cols = slice(k * 128, k * 128 + 128)
                out_ref[q, r * BLK : (r + 1) * BLK, k, :] = acc[q, 6 + r, :, cols] + got[
                    q, r // 3, r % 3, :, cols
                ].astype(F32)

    dens_opp(0)
    gx.start_second()
    dens_side(0, 0)
    for copy in osum:
        copy.wait_recv()
    mine64 = rows_of(a * 64, 64)
    og[mine64] = (od[mine64] + sum(orec[n] for n in range(7))).astype(BF16)
    ogat = [
        remote(osend, orecv, 7 + d - 1, og.at[mine64], og.at[mine64], ao_peers[d - 1])
        for d in range(1, 8)
    ]
    for copy in ogat:
        copy.start()
    add_side(0, 0)
    dens_side(1, 0)
    add_side(1, 0)
    dens_own(0)
    dens_opp(1)
    gx.forward()
    dens_side(0, 1)
    to_z(0)
    dens_side(1, 1)
    add_side(0, 1)
    add_side(1, 1)

    def spread_row(row):
        return jnp.broadcast_to(row, (BLK, BLK))

    for b in range(4):
        square = None
        for k in range(3):
            along = spread_row(coords_ref[k, b : b + 1, :])
            differ = along.T - along
            square = differ * differ if square is None else square + differ * differ
        quad = spread_row(weights_ref[b : b + 1, :])
        kern[b] = quad.T * quad / jnp.sqrt(square + 0.25)
    for copy in tables + ogat:
        copy.wait_recv()
    fill = pltpu.make_async_copy(places, table, local)
    fill.start()
    pair(0)
    fill.wait()
    dens_own(1)
    gx.spread()
    panel(0, 0, 0, 0, 4, fresh=True)
    ge[0].forward()
    ge[0].spread()
    to_z(1)
    gx.spread_opposite()
    gx.arrived(4, 7, 8)
    pair(1)
    middle(0)
    ge[1].forward()
    ge[1].spread()
    gx.arrived(9)
    last(0)
    panel(0, 0, 1, 0, 4, fresh=True)
    middle(1)
    last(1)
    finish(0)
    finish(1)
    for gather in [gx] + ge:
        gather.sent()
    for q in (0, 1):
        for copy in to_opp[q] + to_side[q][0] + to_side[q][1] + over[q] + [to_pair[q]]:
            copy.wait_send()
    for copy in tables + ogat + osum:
        copy.wait_send()


def exchange_step(inv, trial, colloc, occupied, coords, weights):
    rows = trial.shape[0]
    hbm = pl.BlockSpec(memory_space=pl.ANY)
    vmem = pl.BlockSpec(memory_space=pltpu.VMEM)
    smem = pl.BlockSpec(memory_space=pltpu.SMEM)
    return pl.pallas_call(
        main_kernel,
        out_shape=jax.ShapeDtypeStruct((2, 6 * BLK, 2, NOCC), F32),
        in_specs=[smem, hbm, vmem, vmem, vmem, vmem, vmem],
        out_specs=vmem,
        scratch_shapes=[
            *[pltpu.VMEM((4, SIG + 1, BLK, BLK), BF16)] * 8,
            pltpu.VMEM((4, SIG + 1, BLK, BLK), BF16),
            pltpu.VMEM((2, 4, 4, BLK, 256), BF16),
            pltpu.VMEM((2, 4, 4, BLK, 256), BF16),
            pltpu.VMEM((2, 4) + inv.shape, jnp.int32),
            pltpu.SMEM((2, 4) + inv.shape, jnp.int32),
            pltpu.VMEM((4, BLK, BLK), F32),
            pltpu.VMEM((2, 12, BLK, 256), F32),
            pltpu.VMEM((2, 2, 3, BLK, 256), BF16),
            pltpu.VMEM((2, 2, 3, BLK, 256), BF16),
            pltpu.VMEM((16, rows, 2, NOCC), BF16),
            pltpu.VMEM((rows, 256), BF16),
            pltpu.VMEM((ROWS, rows), BF16),
            pltpu.VMEM((2, ROWS, 512), BF16),
            pltpu.VMEM((2, 2, ROWS, 512), BF16),
            pltpu.VMEM((2, ROWS, 512), F32),
            pltpu.VMEM((2, ROWS, 512), BF16),
            pltpu.VMEM((2, 2, ROWS, 512), BF16),
            pltpu.VMEM((2, ROWS, 256), BF16),
            pltpu.VMEM((2, ROWS, 256), BF16),
            pltpu.VMEM((ROWS, 256), BF16),
            pltpu.VMEM((ROWS, 2 * NOCC), F32),
            pltpu.VMEM((7, ROWS // 8, 2 * NOCC), F32),
            pltpu.VMEM((ROWS, 2 * NOCC), BF16),
            pltpu.SemaphoreType.DMA((16,)),
            pltpu.SemaphoreType.DMA((14,)),
            pltpu.SemaphoreType.DMA((14,)),
            pltpu.SemaphoreType.DMA((14,)),
            pltpu.SemaphoreType.DMA((14,)),
            pltpu.SemaphoreType.DMA((37,)),
            pltpu.SemaphoreType.DMA((37,)),
            pltpu.SemaphoreType.DMA((4,)),
            pltpu.SemaphoreType.DMA((4,)),
            pltpu.SemaphoreType.DMA,
        ],
        compiler_params=pltpu.CompilerParams(
            vmem_limit_bytes=63 << 20, collective_id=0, has_side_effects=True
        ),
        name="exchange_step",
    )(inv, trial, colloc, occupied, inv, coords, weights)


def place_of(ids, wanted):
    hit = ids[..., None, :] == wanted[..., :, None]
    where = jnp.arange(SIG, dtype=jnp.int32)
    return SIG + jnp.sum(jnp.where(hit, where - SIG, 0), axis=-1).astype(jnp.int32)


def on_device(trial, occupied, colloc, blocks, coords, weights):
    nblk = trial.shape[0] // BLK * lax.axis_size("ao")
    inv = place_of(blocks, jnp.arange(nblk, dtype=jnp.int32))
    inv = jnp.pad(inv, ((0, 4), (0, BLK - nblk)))
    return exchange_step(inv, trial, colloc, occupied, coords.transpose(1, 0, 2), weights)


def solution(mesh):
    in_specs = (
        P("ao", None, None, None),
        P("ao", None, None),
        P("grid", None, None),
        P("grid", None),
        P("grid", None, None),
        P("grid", None),
    )
    out_specs = P("ao", "grid", None, None)
    return jax.shard_map(
        on_device, mesh=mesh, in_specs=in_specs, out_specs=out_specs, check_vma=False
    )
```

time: 121 us -> 112 us (0.926); the launches traced: 119 us -> 112 us
  Pallas kernels: 115 us -> 108 us
    pallas_call x1, Pallas kernels: 115 us -> 108 us  [exchange_step(): pl.pallas_call(main_kernel, out_shape=jax.ShapeDtypeStruct((2, 6 * BLK, 2...]
where the time goes in v4:
time: 112 us
  Pallas kernels  108 us (96%)
  local copies, waits for them, and re-layouts  4.02 us (4%)
    pallas_call x1, Pallas kernels, exchange_step(): pl.pallas_call(main_kernel, out_shape=jax.ShapeDtypeStruct((2, 6 * BLK, 2...  108 us
    unnamed x2, local copies, waits for them, and re-layouts  3.42 us

profile of v4, /device:TPU:6, one launch (start us, length us, event | category | flops | bytes accessed | tf_op | source)
XLA Modules:
  0.0 111.8 jit_solution(8517615005766314466)
XLA Ops:
  0.0 0.8 copy.7
  0.8 0.1 select_reduce_fusion
  0.9 0.6 pad.4.inv_ref.place_ref
  1.5 107.7 %exchange_step.1 = f32[2,768,2,128]{3,2,1,0:T(2,128)} custom-call(s32[8,128]{1,0:T(8,128)} %pad.4.inv_ref.place_ref, bf16[1536,16,2,128]{3,2,1,0:T(2,128)(2,1)} %trial_ref.1, bf16[4,128,1536]{2,1,0:T(8,128)(2,1)} %x_ref.1, bf16[1536,2,128]{2,1,0:T(2,128)(2,1)} %occ_ref.1, s32[8,128]{1,0:T(8,128)} %pad.4.inv_ref.place_ref, f32[3,4,128]{2,1,0:T(4,128)} %bitcast.1, ...), custom_call_target="tpu_custom_call" | custom-call | tf_op jit(solution)/shard_map/exchange_step/pallas_call | solution.py:439
  109.2 2.7 %copy.9 = f32[2,768,2,128]{3,2,1,0:T(2,128)} copy(f32[2,768,2,128]{3,2,1,0:T(2,128)} %exchange_step.1) | data formatting | bytes 3145728
  (2 shorter events, 0.0 us)

commit v5 on v4

--- a/solution.py
+++ b/solution.py
@@ -170,9 +170,6 @@
     for copy in osum:
         copy.start()
 
-    for b in range(4):
-        for n in range(SIG):
-            x00[b, n] = x_ref[b, :, n * BLK : (n + 1) * BLK].T
     xs = [[x00, x01, x02, x03], [x10, x11, x12, x13]]
     es = [e0, e1]
     gx = GatherY(x00, lambda i, slot: xs[i][slot], 0, 4, 0, gsend, grecv, (pl.ds(0, SIG),))
@@ -180,7 +177,6 @@
         GatherY(es[q].at[0, 0], lambda i, slot, q=q: es[q].at[i, slot], 0, 4, 10 + 10 * q, gsend, grecv)
         for q in (0, 1)
     ]
-    gx.start_first()
     tables = [
         remote(gsend, grecv, 30 + n, place_ref, places.at[i, slot], peer)
         for n, (peer, i, slot) in enumerate(grid_peers)
@@ -362,7 +358,10 @@
                 ].astype(F32)
 
     dens_opp(0)
-    gx.start_second()
+    for b in range(4):
+        for n in range(SIG):
+            x00[b, n] = x_ref[b, :, n * BLK : (n + 1) * BLK].T
+    gx.start_first()
     dens_side(0, 0)
     for copy in osum:
         copy.wait_recv()
@@ -379,12 +378,13 @@
     add_side(1, 0)
     dens_own(0)
     dens_opp(1)
-    gx.forward()
     dens_side(0, 1)
-    to_z(0)
     dens_side(1, 1)
     add_side(0, 1)
     add_side(1, 1)
+    gx.forward()
+    gx.start_second()
+    to_z(0)
 
     def spread_row(row):
         return jnp.broadcast_to(row, (BLK, BLK))
@@ -404,14 +404,14 @@
     pair(0)
     fill.wait()
     dens_own(1)
-    gx.spread()
     panel(0, 0, 0, 0, 4, fresh=True)
+    to_z(1)
     ge[0].forward()
     ge[0].spread()
-    to_z(1)
+    pair(1)
+    gx.spread()
     gx.spread_opposite()
     gx.arrived(4, 7, 8)
-    pair(1)
     middle(0)
     ge[1].forward()
     ge[1].spread()

time: 112 us -> 130 us (1.16)
  the two profiles are of different devices: /device:TPU:6 before, /device:TPU:7 now
where the time goes in v5:
time: 130 us
  Pallas kernels  125 us (96%)
  local copies, waits for them, and re-layouts  4.02 us (3%)
    pallas_call x1, Pallas kernels, exchange_step(): pl.pallas_call(main_kernel, out_shape=jax.ShapeDtypeStruct((2, 6 * BLK, 2...  125 us
    unnamed x2, local copies, waits for them, and re-layouts  3.42 us

profile of v5, /device:TPU:7, one launch (start us, length us, event | category | flops | bytes accessed | tf_op | source)
XLA Modules:
  0.0 129.6 jit_solution(8681484850384153330)
XLA Ops:
  0.0 0.8 copy.7
  0.8 0.1 select_reduce_fusion
  0.9 0.6 pad.4.inv_ref.place_ref
  1.5 125.4 %exchange_step.1 = f32[2,768,2,128]{3,2,1,0:T(2,128)} custom-call(s32[8,128]{1,0:T(8,128)} %pad.4.inv_ref.place_ref, bf16[1536,16,2,128]{3,2,1,0:T(2,128)(2,1)} %trial_ref.1, bf16[4,128,1536]{2,1,0:T(8,128)(2,1)} %x_ref.1, bf16[1536,2,128]{2,1,0:T(2,128)(2,1)} %occ_ref.1, s32[8,128]{1,0:T(8,128)} %pad.4.inv_ref.place_ref, f32[3,4,128]{2,1,0:T(4,128)} %bitcast.1, ...), custom_call_target="tpu_custom_call" | custom-call | tf_op jit(solution)/shard_map/exchange_step/pallas_call | solution.py:439
  126.9 2.7 %copy.9 = f32[2,768,2,128]{3,2,1,0:T(2,128)} copy(f32[2,768,2,128]{3,2,1,0:T(2,128)} %exchange_step.1) | data formatting | bytes 3145728
  (2 shorter events, 0.0 us)

commit v6 on v5

--- a/solution.py
+++ b/solution.py
@@ -141,6 +141,13 @@
     ]
     greet(ao_peers + [peer for peer, _, _ in grid_peers] + [beyond])
 
+    xs = [[x00, x01, x02, x03], [x10, x11, x12, x13]]
+    gx = GatherY(x00, lambda i, slot: xs[i][slot], 0, 4, 0, gsend, grecv, (pl.ds(0, SIG),))
+    for b in range(4):
+        for n in range(SIG):
+            x00[b, n] = x_ref[b, :, n * BLK : (n + 1) * BLK].T
+    gx.start_first()
+
     def split(src):
         def some(k, _):
             k = pl.ds(pl.multiple_of(k * 256, 256), 256)
@@ -170,9 +177,7 @@
     for copy in osum:
         copy.start()
 
-    xs = [[x00, x01, x02, x03], [x10, x11, x12, x13]]
     es = [e0, e1]
-    gx = GatherY(x00, lambda i, slot: xs[i][slot], 0, 4, 0, gsend, grecv, (pl.ds(0, SIG),))
     ge = [
         GatherY(es[q].at[0, 0], lambda i, slot, q=q: es[q].at[i, slot], 0, 4, 10 + 10 * q, gsend, grecv)
         for q in (0, 1)
@@ -358,10 +363,6 @@
                 ].astype(F32)
 
     dens_opp(0)
-    for b in range(4):
-        for n in range(SIG):
-            x00[b, n] = x_ref[b, :, n * BLK : (n + 1) * BLK].T
-    gx.start_first()
     dens_side(0, 0)
     for copy in osum:
         copy.wait_recv()
@@ -376,14 +377,14 @@
     add_side(0, 0)
     dens_side(1, 0)
     add_side(1, 0)
+    gx.forward()
+    gx.start_second()
     dens_own(0)
     dens_opp(1)
     dens_side(0, 1)
     dens_side(1, 1)
     add_side(0, 1)
     add_side(1, 1)
-    gx.forward()
-    gx.start_second()
     to_z(0)
 
     def spread_row(row):

time: 130 us -> 115 us (0.88)
  the two profiles are of different devices: /device:TPU:7 before, /device:TPU:1 now
where the time goes in v6:
time: 115 us
  Pallas kernels  111 us (97%)
  local copies, waits for them, and re-layouts  4.02 us (3%)
    pallas_call x1, Pallas kernels, exchange_step(): pl.pallas_call(main_kernel, out_shape=jax.ShapeDtypeStruct((2, 6 * BLK, 2...  111 us
    unnamed x2, local copies, waits for them, and re-layouts  3.42 us

profile of v6, /device:TPU:1, one launch (start us, length us, event | category | flops | bytes accessed | tf_op | source)
XLA Modules:
  0.0 114.9 jit_solution(13479006672376475825)
XLA Ops:
  0.0 0.8 copy.7
  0.8 0.1 select_reduce_fusion
  0.9 0.6 pad.4.inv_ref.place_ref
  1.5 110.8 %exchange_step.1 = f32[2,768,2,128]{3,2,1,0:T(2,128)} custom-call(s32[8,128]{1,0:T(8,128)} %pad.4.inv_ref.place_ref, bf16[1536,16,2,128]{3,2,1,0:T(2,128)(2,1)} %trial_ref.1, bf16[4,128,1536]{2,1,0:T(8,128)(2,1)} %x_ref.1, bf16[1536,2,128]{2,1,0:T(2,128)(2,1)} %occ_ref.1, s32[8,128]{1,0:T(8,128)} %pad.4.inv_ref.place_ref, f32[3,4,128]{2,1,0:T(4,128)} %bitcast.1, ...), custom_call_target="tpu_custom_call" | custom-call | tf_op jit(solution)/shard_map/exchange_step/pallas_call | solution.py:440
  112.3 2.7 %copy.9 = f32[2,768,2,128]{3,2,1,0:T(2,128)} copy(f32[2,768,2,128]{3,2,1,0:T(2,128)} %exchange_step.1) | data formatting | bytes 3145728
  (2 shorter events, 0.0 us)

commit v7 on v6

--- a/solution.py
+++ b/solution.py
@@ -147,6 +147,7 @@
         for n in range(SIG):
             x00[b, n] = x_ref[b, :, n * BLK : (n + 1) * BLK].T
     gx.start_first()
+    gx.start_second()
 
     def split(src):
         def some(k, _):
@@ -377,15 +378,14 @@
     add_side(0, 0)
     dens_side(1, 0)
     add_side(1, 0)
-    gx.forward()
-    gx.start_second()
     dens_own(0)
     dens_opp(1)
+    gx.forward()
     dens_side(0, 1)
+    to_z(0)
     dens_side(1, 1)
     add_side(0, 1)
     add_side(1, 1)
-    to_z(0)
 
     def spread_row(row):
         return jnp.broadcast_to(row, (BLK, BLK))
@@ -405,14 +405,14 @@
     pair(0)
     fill.wait()
     dens_own(1)
+    gx.spread()
     panel(0, 0, 0, 0, 4, fresh=True)
-    to_z(1)
     ge[0].forward()
     ge[0].spread()
-    pair(1)
-    gx.spread()
+    to_z(1)
     gx.spread_opposite()
     gx.arrived(4, 7, 8)
+    pair(1)
     middle(0)
     ge[1].forward()
     ge[1].spread()

time: 115 us -> 109 us (0.948)
  the two profiles are of different devices: /device:TPU:1 before, /device:TPU:6 now
where the time goes in v7:
time: 109 us
  Pallas kernels  105 us (96%)
  local copies, waits for them, and re-layouts  4.02 us (4%)
    pallas_call x1, Pallas kernels, exchange_step(): pl.pallas_call(main_kernel, out_shape=jax.ShapeDtypeStruct((2, 6 * BLK, 2...  105 us
    unnamed x2, local copies, waits for them, and re-layouts  3.42 us

profile of v7, /device:TPU:6, one launch (start us, length us, event | category | flops | bytes accessed | tf_op | source)
XLA Modules:
  0.0 109.2 jit_solution(6560379205655731822)
XLA Ops:
  0.0 0.8 copy.7
  0.8 0.1 select_reduce_fusion
  0.9 0.6 pad.4.inv_ref.place_ref
  1.5 105.0 %exchange_step.1 = f32[2,768,2,128]{3,2,1,0:T(2,128)} custom-call(s32[8,128]{1,0:T(8,128)} %pad.4.inv_ref.place_ref, bf16[1536,16,2,128]{3,2,1,0:T(2,128)(2,1)} %trial_ref.1, bf16[4,128,1536]{2,1,0:T(8,128)(2,1)} %x_ref.1, bf16[1536,2,128]{2,1,0:T(2,128)(2,1)} %occ_ref.1, s32[8,128]{1,0:T(8,128)} %pad.4.inv_ref.place_ref, f32[3,4,128]{2,1,0:T(4,128)} %bitcast.1, ...), custom_call_target="tpu_custom_call" | custom-call | tf_op jit(solution)/shard_map/exchange_step/pallas_call | solution.py:440
  106.5 2.7 %copy.9 = f32[2,768,2,128]{3,2,1,0:T(2,128)} copy(f32[2,768,2,128]{3,2,1,0:T(2,128)} %exchange_step.1) | data formatting | bytes 3145728
  (2 shorter events, 0.0 us)
